TPU v7x, 32 devices: a whole 2x2x4 slice. The times are simulated.
32 devices in a mesh: layer: 4 (over x, core), latent: 8 (over z, y).
Axes of the slice: x: 2, y: 2, z: 4, core: 2. Of those that a mesh axis runs over, the one named last changes fastest.
Arguments:
- acts: bfloat16 [4, 512, 2048], P('layer', None, 'latent'), may hold values from -6 to 6
- w_enc: bfloat16 [4, 2048, 4096], P('layer', None, 'latent'), may hold values from -0.0625 to 0.0625
- b_enc: float32 [4096], P('latent'), may hold values from -3 to 3
- w_dec: bfloat16 [4, 4096, 2048], P('layer', 'latent'), may hold values from -0.125 to 0.125
- b_dec: bfloat16 [4, 2048], P('layer', 'latent'), may hold values from -3 to 3
Outputs:
- grad_enc: bfloat16 [4, 2048, 4096], P('layer', None, 'latent')
- grad_dec: bfloat16 [4, 4096, 2048], P('layer', 'latent')
- grad_benc: float32 [4096], P('latent')
- grad_bdec: float32 [4, 2048], P('layer', 'latent')
All inputs are finite; a program needn't handle non-finite values.
Results may differ from a plain program's by a relative error of at most 0.014.
Values may be sent and summed in bfloat16 or wider, within the bound.
A program may use at most 64 MiB of HBM per device.

v0:
```python
import functools

import jax
import jax.numpy as jnp
from jax import lax
from jax.experimental import pallas as pl
from jax.experimental.pallas import tpu as pltpu
from jax.sharding import PartitionSpec as P

MESH = pl.DeviceIdType.MESH
F32 = jnp.float32
BF16 = jnp.bfloat16
INNER = 2


def place(n):
    me = lax.axis_index("latent")
    return me // INNER, lax.rem(me, INNER), n // INNER


def greet(n):
    z, y, depth = place(n)
    barrier = pltpu.get_barrier_semaphore()

    def signal(index):
        pl.semaphore_signal(barrier, inc=1, device_id={"latent": index}, device_id_type=MESH)

    signal(z * INNER + 1 - y)

    @pl.when(z > 0)
    def _():
        signal((z - 1) * INNER + y)

    @pl.when(z < depth - 1)
    def _():
        signal((z + 1) * INNER + y)

    peers = 1 + jnp.where(z > 0, 1, 0) + jnp.where(z < depth - 1, 1, 0)
    pl.semaphore_wait(barrier, peers)


def remote(src, dst, send, recv, index, axis="latent"):
    return pltpu.make_async_remote_copy(
        src_ref=src,
        dst_ref=dst,
        send_sem=send,
        recv_sem=recv,
        device_id={axis: index},
        device_id_type=MESH,
    )


def gather_kernel(n, view_in, view, x_ref, out_ref, local_sem, send, recv):
    z, y, depth = place(n)
    greet(n)
    me = z * INNER + y
    partner = z * INNER + 1 - y

    def move(h, block, way, own, start):
        src = view_in(x_ref, h) if own else view(out_ref, block, h)
        target = (partner, me + INNER, me - INNER)[way]
        copy = remote(src, view(out_ref, block, h), send.at[way, h, block], recv.at[h, block], target)
        if start:
            copy.start()
        else:
            copy.wait_send()

    def along(h, block, own, start, up=True, down=True):
        if up:

            @pl.when(z < depth - 1)
            def _():
                move(h, block, 1, own, start)

        if down:

            @pl.when(z > 0)
            def _():
                move(h, block, 2, own, start)

    def arrive(h, block):
        spot = view(out_ref, block, h)
        remote(spot, spot, send.at[0, h, block], recv.at[h, block], partner).wait_recv()

    def run(start):
        move(1, me, 0, True, start)
        along(0, me, True, start)
        along(1, me, True, start)
        move(0, me, 0, True, start)
        if start:
            keep = [
                pltpu.make_async_copy(view_in(x_ref, h), view(out_ref, me, h), local_sem.at[h])
                for h in range(2)
            ]
            for copy in keep:
                copy.start()
            arrive(1, partner)
        along(1, partner, False, start)
        for d in range(1, depth):
            for below in (True, False):
                at = z - d if below else z + d

                @pl.when(at >= 0 if below else at < depth)
                def _():
                    for h, side in ((0, y), (1, y), (1, 1 - y)):
                        block = at * INNER + side
                        if start:
                            arrive(h, block)
                        along(h, block, False, start, up=below, down=not below)
                        if h == 0:
                            move(0, block, 0, False, start)

        if start:
            for copy in keep:
                copy.wait()
            for at in range(depth):
                arrive(0, at * INNER + 1 - y)

    run(True)
    run(False)


def gather_blocks(x, n, by_rows, collective_id):
    rows, width = x.shape
    if by_rows:
        shape, half = (n * rows, width), width // 2
        flat = rows % 16 == 0 and half % 128 == 0
        blocks = (rows, half)
        view_in = lambda ref, h: ref.at[:, pl.ds(h * half, half)]
        view = lambda ref, j, h: ref.at[
            pl.ds(pl.multiple_of(j * rows, rows), rows), pl.ds(h * half, half)
        ]
    else:
        shape, half = (rows, n * width), rows // 2
        flat = width % 128 == 0 and half % 16 == 0
        blocks = (half, width)
        view_in = lambda ref, h: ref.at[pl.ds(h * half, half), :]
        view = lambda ref, j, h: ref.at[
            pl.ds(h * half, half), pl.ds(pl.multiple_of(j * width, width), width)
        ]
    if not flat:
        if by_rows:
            x = x.reshape(rows, 2, half).transpose(1, 0, 2)
        else:
            x = x.reshape(2, half, width)
        shape = (n, 2) + blocks
        view_in = lambda ref, h: ref.at[h]
        view = lambda ref, j, h: ref.at[j, h]
    out = pl.pallas_call(
        functools.partial(gather_kernel, n, view_in, view),
        out_shape=jax.ShapeDtypeStruct(shape, x.dtype),
        in_specs=[pl.BlockSpec(memory_space=pltpu.VMEM)],
        out_specs=pl.BlockSpec(memory_space=pltpu.VMEM),
        scratch_shapes=[
            pltpu.SemaphoreType.DMA((2,)),
            pltpu.SemaphoreType.DMA((3, 2, n)),
            pltpu.SemaphoreType.DMA((2, n)),
        ],
        compiler_params=pltpu.CompilerParams(collective_id=collective_id, has_side_effects=True),
        name="gather_rows" if by_rows else "gather_columns",
    )(x)
    if flat:
        return out
    if by_rows:
        return out.transpose(0, 2, 1, 3).reshape(n * rows, width)
    return out.transpose(1, 2, 0, 3).reshape(rows, n * width)


def scatter_kernel(
    n, view, part, out_ref, side_in, up_in, down_in, up_out, down_out, last_in, last_out,
    side_sem, up_sem, down_sem, last_sem,
):
    z, y, depth = place(n)
    greet(n)
    me = z * INNER + y
    partner = z * INNER + 1 - y

    def side_copy(at):
        return remote(
            view(part, at * INNER + 1 - y, 0), side_in.at[at],
            side_sem.at[0, at], side_sem.at[1, at], partner,
        )

    def line_copy(up, lane, at):
        stay, land, sems = (up_out, up_in, up_sem) if up else (down_out, down_in, down_sem)
        return remote(
            stay.at[lane, at], land.at[lane, at], sems.at[0, lane, at], sems.at[1, lane, at],
            me + INNER if up else me - INNER,
        )

    last_copy = remote(last_out, last_in, last_sem.at[0], last_sem.at[1], partner)

    for at in range(depth):
        side_copy(at).start()

    def own_term(lane, at):
        if lane < 2:
            return view(part, at * INNER + lane, 1)[...].astype(F32)
        return view(part, at * INNER + y, 0)[...].astype(F32) + side_in[at].astype(F32)

    for d in range(depth - 1, 0, -1):
        for lane in range(3):
            if lane == 2:
                for up in (True, False):
                    at = z + d if up else z - d

                    @pl.when(at < depth if up else at >= 0)
                    def _():
                        side_copy(at).wait_recv()

            for up in (True, False):
                at = z + d if up else z - d
                valid = at < depth if up else at >= 0
                inner = z > 0 if up else z < depth - 1
                stay, land = (up_out, up_in) if up else (down_out, down_in)

                @pl.when(jnp.logical_and(valid, inner))
                def _():
                    line_copy(up, lane, at).wait_recv()
                    stay[lane, at] = (own_term(lane, at) + land[lane, at].astype(F32)).astype(BF16)

                @pl.when(jnp.logical_and(valid, jnp.logical_not(inner)))
                def _():
                    stay[lane, at] = own_term(lane, at).astype(BF16)

                @pl.when(valid)
                def _():
                    line_copy(up, lane, at).start()

    side_copy(z).wait_recv()

    @pl.when(z > 0)
    def _():
        for lane in range(3):
            line_copy(True, lane, z).wait_recv()

    @pl.when(z == 0)
    def _():
        for lane in range(3):
            up_in[lane, z] = jnp.zeros(up_in.shape[2:], BF16)

    @pl.when(z < depth - 1)
    def _():
        for lane in range(3):
            line_copy(False, lane, z).wait_recv()

    @pl.when(z == depth - 1)
    def _():
        for lane in range(3):
            down_in[lane, z] = jnp.zeros(down_in.shape[2:], BF16)

    def both(lane):
        return up_in[lane, z].astype(F32) + down_in[lane, z].astype(F32)

    other = 1 - y
    last_out[...] = (view(part, partner, 1)[...].astype(F32) + both(other)).astype(BF16)
    last_copy.start()
    out_ref[0] = own_term(2, z) + both(2)
    last_copy.wait_recv()
    out_ref[1] = view(part, me, 1)[...].astype(F32) + both(y) + last_in[...].astype(F32)
    last_copy.wait_send()
    for at in range(depth):
        side_copy(at).wait_send()
    for d in range(depth - 1, 0, -1):
        for up in (True, False):
            at = z + d if up else z - d

            @pl.when(at < depth if up else at >= 0)
            def _():
                for lane in range(3):
                    line_copy(up, lane, at).wait_send()


def scatter_sum(x, n, collective_id):
    tokens, width = x.shape
    rows, half, depth = tokens // n, width // 2, n // INNER
    flat = rows % 16 == 0 and half % 128 == 0
    if flat:
        view = lambda ref, j, h: ref.at[
            pl.ds(pl.multiple_of(j * rows, rows), rows), pl.ds(h * half, half)
        ]
    else:
        x = x.reshape(n, rows, 2, half).transpose(0, 2, 1, 3)
        view = lambda ref, j, h: ref.at[j, h]
    line = pltpu.VMEM((3, depth, rows, half), BF16)
    out = pl.pallas_call(
        functools.partial(scatter_kernel, n, view),
        out_shape=jax.ShapeDtypeStruct((2, rows, half), F32),
        in_specs=[pl.BlockSpec(memory_space=pltpu.VMEM)],
        out_specs=pl.BlockSpec(memory_space=pltpu.VMEM),
        scratch_shapes=[
            pltpu.VMEM((depth, rows, half), BF16),
            line, line, line, line,
            pltpu.VMEM((rows, half), BF16),
            pltpu.VMEM((rows, half), BF16),
            pltpu.SemaphoreType.DMA((2, depth)),
            pltpu.SemaphoreType.DMA((2, 3, depth)),
            pltpu.SemaphoreType.DMA((2, 3, depth)),
            pltpu.SemaphoreType.DMA((2,)),
        ],
        compiler_params=pltpu.CompilerParams(collective_id=collective_id, has_side_effects=True),
        name="scatter_sum",
    )(x)
    return jnp.concatenate([out[0], out[1]], axis=1)


def reduce_kernel(part, out_ref, pair_in, far_in, far_out, sems):
    place_own = lax.axis_index("layer")
    core = lax.rem(place_own, 2)
    pair = place_own + 1 - 2 * core
    far = lax.rem(place_own + 2, 4)
    barrier = pltpu.get_barrier_semaphore()
    for index in (pair, far):
        pl.semaphore_signal(barrier, inc=1, device_id={"layer": index}, device_id_type=MESH)
    pl.semaphore_wait(barrier, 2)
    first = remote(part.at[1 - core], pair_in, sems.at[0], sems.at[1], pair, "layer")
    first.start()
    first.wait_recv()
    far_out[...] = (part[core].astype(F32) + pair_in[...].astype(F32)).astype(BF16)
    second = remote(far_out, far_in, sems.at[2], sems.at[3], far, "layer")
    second.start()
    second.wait_recv()
    out_ref[core] = (far_out[...].astype(F32) + far_in[...].astype(F32)).astype(BF16)
    third = remote(out_ref.at[core], out_ref.at[core], sems.at[4], sems.at[5], pair, "layer")
    third.start()
    third.wait_recv()
    first.wait_send()
    second.wait_send()
    third.wait_send()


def layer_sum(x, collective_id):
    tokens, width = x.shape
    half = tokens // 2
    out = pl.pallas_call(
        reduce_kernel,
        out_shape=jax.ShapeDtypeStruct((2, half, width), BF16),
        in_specs=[pl.BlockSpec(memory_space=pltpu.VMEM)],
        out_specs=pl.BlockSpec(memory_space=pltpu.VMEM),
        scratch_shapes=[pltpu.VMEM((half, width), BF16)] * 3 + [pltpu.SemaphoreType.DMA((6,))],
        compiler_params=pltpu.CompilerParams(collective_id=collective_id, has_side_effects=True),
        name="layer_sum",
    )(x.reshape(2, half, width))
    return out.reshape(tokens, width).astype(F32)


def body(n, acts, w_enc, b_enc, w_dec, b_dec):
    local = acts[0]
    width_own = local.shape[1]
    enc_own = w_enc[0]
    dec_own = w_dec[0]
    full = gather_blocks(local, n, False, 0)
    tokens_all = full.shape[0]
    scale = tokens_all ** (-0.5)
    position = lax.axis_index("latent")
    rows = tokens_all // n
    part = jnp.dot(full, enc_own, preferred_element_type=F32).astype(BF16)
    pre = layer_sum(part, 1) + b_enc[None, :]
    feat = (jax.nn.softplus(4.0 * pre) / 4.0).astype(BF16)
    bias_own = lax.dynamic_update_slice(
        jnp.zeros((1, n * width_own), F32), b_dec.astype(F32), (0, position * width_own)
    )
    term = jnp.dot(feat, dec_own, preferred_element_type=F32) + bias_own
    recon = scatter_sum(term.astype(BF16), n, 2)
    own_rows = lax.dynamic_slice_in_dim(full, position * rows, rows, 0)
    err_rows = (recon - own_rows.astype(F32)).astype(BF16)
    err = gather_blocks(err_rows, n, True, 3)
    bias_grad_full = scale * jnp.sum(err.astype(F32), axis=0)
    grad_bdec = lax.dynamic_slice_in_dim(bias_grad_full, position * width_own, width_own, 0)
    dec_prod = lax.dot_general(
        feat, err, (((0,), (0,)), ((), ())), preferred_element_type=F32
    )
    grad_dec = (scale * dec_prod).astype(BF16)
    feat_term = lax.dot_general(
        err, dec_own, (((1,), (1,)), ((), ())), preferred_element_type=F32
    )
    grad_feat = scale * layer_sum(feat_term.astype(BF16), 4)
    grad_pre = grad_feat * jax.nn.sigmoid(4.0 * pre)
    grad_benc = jnp.sum(grad_pre, axis=0)
    grad_pre_b = grad_pre.astype(BF16)
    enc_prod = lax.dot_general(
        full, grad_pre_b, (((0,), (0,)), ((), ())), preferred_element_type=F32
    )
    grad_enc = enc_prod.astype(BF16)
    return (grad_enc[None], grad_dec[None], grad_benc, grad_bdec[None])


def solution(mesh):
    return jax.shard_map(
        functools.partial(body, mesh.shape["latent"]),
        mesh=mesh,
        in_specs=(
            P("layer", None, "latent"),
            P("layer", None, "latent"),
            P("latent"),
            P("layer", "latent", None),
            P("layer", "latent"),
        ),
        out_specs=(
            P("layer", None, "latent"),
            P("layer", "latent", None),
            P("latent"),
            P("layer", "latent"),
        ),
        check_vma=False,
    )
```

profile of v0, /device:TPU:0, one launch (start us, length us, event | category | flops | bytes accessed | tf_op | source)
XLA Modules:
  0.0 163.7 jit_solution(545478676106481197)
XLA Ops:
  0.6 0.0 copy-start
  0.6 34.2 %gather_columns.1 = bf16[512,2048]{1,0:T(8,128)(2,1)} custom-call(bf16[512,256]{1,0:T(8,128)(2,1)} %bitcast.50), custom_call_target="tpu_custom_call" | custom-call | tf_op jit(solution)/shard_map/gather_columns/pallas_call | solution.py:149
  34.8 0.0 copy-start.4
  34.8 4.3 %fusion.7 = bf16[512,512]{1,0:T(8,128)(2,1)} fusion(bf16[512,2048]{1,0:T(8,128)(2,1)} %gather_columns.1, bf16[1,2048,512]{2,1,0:T(8,128)(2,1)} %param.6), kind=kOutput, calls=%fused_computation.13 | convolution fusion | flops 1074003968 | bytes 4718592 | tf_op jit(solution)/shard_map/dot_general | solution.py:357
  39.1 0.0 copy-start.5
  39.1 13.2 %layer_sum.2 = bf16[2,256,512]{2,1,0:T(8,128)(2,1)} custom-call(bf16[2,256,512]{2,1,0:T(8,128)(2,1)} %bitcast.48), custom_call_target="tpu_custom_call" | custom-call | tf_op jit(solution)/shard_map/layer_sum/pallas_call | solution.py:335
  52.4 0.0 copy-done.4
  52.4 1.8 %fusion.14 = bf16[2,256,512]{2,1,0:T(8,128)(2,1)S(1)} fusion(bf16[2,256,512]{2,1,0:T(8,128)(2,1)} %layer_sum.2, f32[512]{0:T(512)S(1)} %copy-done.4), kind=kLoop, calls=%fused_computation.16 | loop fusion | flops 2883584 | bytes 1050624 | tf_op jit(solution)/shard_map/convert_element_type | solution.py:359
  54.1 0.0 copy-done.5
  54.2 0.3 dynamic_update_slice.4
  54.5 0.0 copy-done
  54.5 2.6 %add_convert_fusion.part = bf16[512,2048]{1,0:T(8,128)(2,1)} fusion(bf16[512,512]{1,0:T(8,128)(2,1)S(1)} %bitcast.47, bf16[1,512,2048]{2,1,0:T(8,128)(2,1)S(1)} %copy-done, f32[2048]{0:T(1024)S(1)} %dynamic_update_slice.4), kind=kOutput, calls=%fused_computation.2 | convolution fusion | flops 1075838976 | bytes 4726784 | tf_op jit(solution)/shard_map/dot_general | solution.py:363
  57.0 39.1 %scatter_sum.1 = f32[2,64,1024]{2,1,0:T(8,128)} custom-call(bf16[512,2048]{1,0:T(8,128)(2,1)} %add_convert_fusion.part), custom_call_target="tpu_custom_call" | custom-call | tf_op jit(solution)/shard_map/scatter_sum/pallas_call | solution.py:286
  96.2 1.1 slice_bitcast_fusion.1
  97.2 1.7 %fusion.19.x_ref = bf16[64,2048]{1,0:T(8,128)(2,1)} fusion(f32[64,1024]{1,0:T(8,128)S(1)} %get-tuple-element.13, f32[64,1024]{1,0:T(8,128)S(1)} %get-tuple-element.12, bf16[512,2048]{1,0:T(8,128)(2,1)} %gather_columns.1, s32[]{:T(128)S(6)} %select_n.16), kind=kLoop, calls=%fused_computation.27 | loop fusion | flops 524288 | bytes 1048580 | tf_op jit(solution)/shard_map/convert_element_type | solution.py:366
  98.9 33.9 %gather_rows.1 = bf16[512,2048]{1,0:T(8,128)(2,1)} custom-call(bf16[64,2048]{1,0:T(8,128)(2,1)} %fusion.19.x_ref), custom_call_target="tpu_custom_call" | custom-call | tf_op jit(solution)/shard_map/gather_rows/pallas_call | solution.py:149
  132.8 0.0 copy-start.2
  132.9 3.7 %fusion.10 = bf16[512,512]{1,0:T(8,128)(2,1)} fusion(bf16[512,2048]{1,0:T(8,128)(2,1)} %gather_rows.1, bf16[1,512,2048]{2,1,0:T(8,128)(2,1)S(1)} %copy-done), kind=kOutput, calls=%fused_computation.14 | convolution fusion | flops 1074003968 | bytes 4718592 | tf_op jit(solution)/shard_map/dot_general | solution.py:374
  136.6 12.1 %layer_sum.3 = bf16[2,256,512]{2,1,0:T(8,128)(2,1)} custom-call(bf16[2,256,512]{2,1,0:T(8,128)(2,1)} %bitcast.49), custom_call_target="tpu_custom_call" | custom-call | tf_op jit(solution)/shard_map/layer_sum/pallas_call | solution.py:335
  148.7 0.0 copy-done.2
  148.7 0.0 copy-start.3
  148.7 2.2 %multiply_reduce_fusion = (f32[512]{0:T(512)}, f32[2,256,512]{2,1,0:T(8,128)S(1)}) fusion(bf16[2,256,512]{2,1,0:T(8,128)(2,1)S(1)} %copy-done.2, f32[512]{0:T(512)S(1)} %copy-done.4, bf16[2,256,512]{2,1,0:T(8,128)(2,1)} %layer_sum.3), kind=kLoop, calls=%fused_computation.23 | loop fusion | flops 2620928 | bytes 2101248 | tf_op jit(solution)/shard_map/reduce_sum | solution.py:379
  150.8 1.0 fusion.16
  151.8 0.0 copy-done.3
  151.8 2.6 %fusion = bf16[1,2048,512]{1,2,0:T(8,128)(2,1)} fusion(bf16[512,512]{1,0:T(8,128)(2,1)S(1)} %get-tuple-element.9, bf16[512,2048]{1,0:T(8,128)(2,1)S(1)} %copy-done.3), kind=kOutput, calls=%fused_computation.6 | convolution fusion | flops 1074790400 | bytes 4718592 | tf_op jit(solution)/shard_map/dot_general | solution.py:381
  154.4 3.9 %copy.9 = bf16[1,2048,512]{2,1,0:T(8,128)(2,1)} copy(bf16[1,2048,512]{1,2,0:T(8,128)(2,1)} %fusion) | data formatting | bytes 4194304
  158.3 0.0 copy-start.1
  158.3 4.3 %fusion.1 = bf16[1,512,2048]{2,1,0:T(8,128)(2,1)} fusion(bf16[512,512]{1,0:T(8,128)(2,1)S(1)} %get-tuple-element.8, bf16[512,2048]{1,0:T(8,128)(2,1)} %gather_rows.1), kind=kOutput, calls=%fused_computation.7 | convolution fusion | flops 1075838976 | bytes 4718592 | tf_op jit(solution)/shard_map/dot_general | solution.py:370
  162.7 0.0 copy-done.1
  162.7 0.4 convert_reduce_fusion
  163.1 0.6 dynamic-slice_multiply_fusion
  (2 shorter events, 0.0 us)
Async XLA Ops:
  0.6 53.8 %copy-start = (bf16[1,512,2048]{2,1,0:T(8,128)(2,1)S(1)}, bf16[1,512,2048]{2,1,0:T(8,128)(2,1)}, u32[]{:S(2)}) copy-start(bf16[1,512,2048]{2,1,0:T(8,128)(2,1)} %param.8) | copy-start | bytes 6291460
  34.8 17.5 %copy-start.4 = (f32[512]{0:T(512)S(1)}, f32[512]{0:T(512)}, u32[]{:S(2)}) copy-start(f32[512]{0:T(512)} %param.7) | copy-start | bytes 6148
  39.1 15.0 %copy-start.5 = (bf16[1,256]{1,0:T(2,128)(2,1)S(1)}, bf16[1,256]{1,0:T(2,128)(2,1)}, u32[]{:S(2)}) copy-start(bf16[1,256]{1,0:T(2,128)(2,1)} %param.9) | copy-start | bytes 1540
  132.8 15.8 %copy-start.2 = (bf16[2,256,512]{2,1,0:T(8,128)(2,1)S(1)}, bf16[2,256,512]{2,1,0:T(8,128)(2,1)}, u32[]{:S(2)}) copy-start(bf16[2,256,512]{2,1,0:T(8,128)(2,1)} %layer_sum.2) | copy-start | bytes 1572868
  148.7 3.1 %copy-start.3 = (bf16[512,2048]{1,0:T(8,128)(2,1)S(1)}, bf16[512,2048]{1,0:T(8,128)(2,1)}, u32[]{:S(2)}) copy-start(bf16[512,2048]{1,0:T(8,128)(2,1)} %gather_columns.1) | copy-start | bytes 6291460
  158.3 4.3 %copy-start.1 = (bf16[512,2048]{1,0:T(8,128)(2,1)S(1)}, bf16[512,2048]{1,0:T(8,128)(2,1)}, u32[]{:S(2)}) copy-start(bf16[512,2048]{1,0:T(8,128)(2,1)} %gather_rows.1) | copy-start | bytes 6291460
where the time goes:
time: 164 us
  Pallas kernels  132 us (80%)
  matrix products  17.5 us (11%)
  other arithmetic  7.63 us (5%)
  local copies, waits for them, and re-layouts  5.3 us (3%)
    pallas_call x2, Pallas kernels, gather_blocks(): pl.pallas_call(functools.partial(gather_kernel, n, view_in, view), out_sh...  68.1 us
    pallas_call x1, Pallas kernels, scatter_sum(): pl.pallas_call(functools.partial(scatter_kernel, n, view), out_shape=jax....  39.1 us
    pallas_call x2, Pallas kernels, layer_sum(): pl.pallas_call(reduce_kernel, out_shape=jax.ShapeDtypeStruct((2, half, wi...  25.3 us
    dot_general x1, matrix products, body(): lax.dot_general(feat, err, (((0,), (0,)), ((), ())), preferred_element_ty...  4.34 us
    dot_general x1, matrix products, body(): part = jnp.dot(full, enc_own, preferred_element_type=F32).astype(BF16)  4.27 us
    unnamed x13, local copies, waits for them, and re-layouts  3.95 us
    dot_general x1, matrix products, body(): lax.dot_general(err, dec_own, (((1,), (1,)), ((), ())), preferred_element...  3.72 us

commit v1 on v0

v1 whole, which is shorter than its diff:
```python
import functools

import jax
import jax.numpy as jnp
from jax import lax
from jax.experimental import pallas as pl
from jax.experimental.pallas import tpu as pltpu
from jax.sharding import PartitionSpec as P

MESH = pl.DeviceIdType.MESH
F32 = jnp.float32
BF16 = jnp.bfloat16
INNER = 2
VMEM_LIMIT = 60 * 1024 * 1024
SHARES = (2, 2, 2, 1, 1)
PLAN = dict(
    direct=(0, 3), act=(0.0, 4.0, 9.0, 13.0, 16.0), act_hop=3.0, use=0.3, gap=(3.0, 3.0),
    out=(16.0, 21.0, 27.0, 33.0, 36.0), out_hop=3.0, near=3.0, err=(0.0,) * 5, err_hop=3.0,
)
SINGLE = dict(
    direct=(), act=(0.0,), act_hop=3.0, use=0.3, gap=(3.0, 3.0),
    out=(0.0,), out_hop=3.0, near=3.0, err=(0.0,), err_hop=3.0,
)


def remote(src, dst, send, recv, axis, index):
    return pltpu.make_async_remote_copy(
        src_ref=src,
        dst_ref=dst,
        send_sem=send,
        recv_sem=recv,
        device_id={axis: index},
        device_id_type=MESH,
    )


def dot(a, b, dims=((1,), (0,))):
    return lax.dot_general(a, b, (dims, ((), ())), preferred_element_type=F32)


def step_kernel(n, sizes, plan, flat, scale, acts_hbm, enc_hbm, dec_hbm, benc_hbm, bdec_hbm, *refs):
    if flat:
        (genc, gdec, gbenc, gbdec), refs = refs[:4], refs[4:]
        (full, err, feat, gpre, turned, feat_turned), refs = refs[:6], refs[6:]
    else:
        (full, err, feat, gpre, gbenc, gbdec), refs = refs[:6], refs[6:]
    (
        enc, dec, benc_ref, bdec_ref, part, own,
        side_out, side_in, line_out, line_in,
        xup_out, xup_in, xdown_out, xdown_in, sum_out, sum_in, total, gate,
        load_sem, ag_send, ag_recv, eg_send, eg_recv,
        side_sem, up_sem, down_sem, xup_sem, xdown_sem, sum_sem,
    ) = refs
    depth = n // INNER
    tokens, width = acts_hbm.shape
    chunks = len(sizes)
    me = lax.axis_index("latent")
    z, y = me // INNER, lax.rem(me, INNER)
    partner = z * INNER + 1 - y
    layer = lax.axis_index("layer")
    peers = 4
    not_top, not_bottom = z < depth - 1, z > 0

    barrier = pltpu.get_barrier_semaphore()

    def greet(axis, index):
        pl.semaphore_signal(barrier, inc=1, device_id={axis: index}, device_id_type=MESH)

    greet("latent", partner)
    pl.when(not_top)(lambda: greet("latent", me + INNER))
    pl.when(not_bottom)(lambda: greet("latent", me - INNER))
    for k in range(1, peers):
        greet("layer", lax.rem(layer + k, peers))
    loads = [
        pltpu.make_async_copy(acts_hbm, full.at[me], load_sem.at[0]),
        pltpu.make_async_copy(benc_hbm, benc_ref, load_sem.at[1]),
        pltpu.make_async_copy(bdec_hbm, bdec_ref, load_sem.at[2]),
        pltpu.make_async_copy(enc_hbm, enc, load_sem.at[3]),
        pltpu.make_async_copy(dec_hbm, dec, load_sem.at[4]),
    ]
    for load in loads:
        load.start()
    pl.semaphore_wait(
        barrier, peers + jnp.where(not_top, 1, 0) + jnp.where(not_bottom, 1, 0)
    )

    gbdec[...] = jnp.zeros_like(gbdec)
    gbenc[...] = jnp.zeros_like(gbenc)

    starts = [sum(sizes[:c]) for c in range(chunks)]

    def span(c):
        return pl.ds(starts[c], sizes[c])

    def direct(c):
        return c in plan["direct"]

    def share(c, peer):
        quarter = sizes[c] // peers
        return pl.ds(pl.multiple_of(starts[c] + peer * quarter, quarter), quarter)

    def slot(c):
        return pl.ds(starts[c] // peers, sizes[c] // peers)

    def enc_rows(b):
        return enc[pl.ds(pl.multiple_of(b * width, width), width), :]

    def dec_columns(b):
        if flat:
            return dec[:, pl.ds(pl.multiple_of(b * width, width), width)]
        return dec[b]

    targets = (partner, me + INNER, me - INNER)

    def gather_copy(buf, send, recv, c, b, way, source=None):
        spot = buf.at[b, span(c), :]
        return remote(
            spot if source is None else source, spot,
            send.at[c, b, way], recv.at[c, b], "latent", targets[way],
        )

    def gather_own(buf, send, recv, c, source, act):
        def go(way):
            act(gather_copy(buf, send, recv, c, me, way, source))

        pl.when(not_top)(lambda: go(1))
        pl.when(not_bottom)(lambda: go(2))
        go(0)

    def gather_line(buf, send, recv, c, d, below, act, wait):
        at = z - d if below else z + d

        @pl.when(at >= 0 if below else at < depth)
        def _():
            b = at * INNER + y
            if wait:
                gather_copy(buf, send, recv, c, b, 0).wait_recv()
            way = 1 if below else 2

            @pl.when(not_top if below else not_bottom)
            def _():
                act(gather_copy(buf, send, recv, c, b, way))

            if not (direct(c) and d == 1):
                act(gather_copy(buf, send, recv, c, b, 0))

    def gather_side(buf, send, recv, c, d, below, act, wait):
        at = z - d if below else z + d

        @pl.when(at >= 0 if below else at < depth)
        def _():
            b = at * INNER + 1 - y
            if wait:
                gather_copy(buf, send, recv, c, b, 0).wait_recv()
            if direct(c) and d == 0:
                for way, valid in ((1, not_top), (2, not_bottom)):

                    @pl.when(valid)
                    def _():
                        act(gather_copy(buf, send, recv, c, b, way))

    def on_block(d, below, side, use):
        at = z - d if below else z + d

        @pl.when(at >= 0 if below else at < depth)
        def _():
            use(at * INNER + (1 - y if side else y))

    def start(copy):
        copy.start()

    def finish(copy):
        copy.wait_send()

    events = []

    def event(time, function, *args):
        events.append((time, len(events), functools.partial(function, *args)))

    def gather_events(buf, send, recv, c, source, time, hop, use):
        event(time, gather_own, buf, send, recv, c, source, start)
        event(time + 0.1, use, c, me)
        for d in range(1, depth):
            for below in (True, False):
                at = time + d * hop
                event(at, gather_line, buf, send, recv, c, d, below, start, True)
                event(at + plan["use"], on_block, d, below, False, functools.partial(use, c))
        for d in range(depth):
            for below in (True, False) if d else (True,):
                at = time + (d + 1) * hop + 0.2
                event(at, gather_side, buf, send, recv, c, d, below, start, True)
                event(at + 0.3, on_block, d, below, True, functools.partial(use, c))
        return time + depth * hop + 0.6

    def gather_finish(buf, send, recv, c, source):
        gather_own(buf, send, recv, c, source, finish)
        for d in range(1, depth):
            for below in (True, False):
                gather_line(buf, send, recv, c, d, below, finish, False)
        gather_side(buf, send, recv, c, 0, True, finish, False)

    def sum_copy(s, c, phase, k):
        peer = lax.rem(layer + k, peers)
        if phase == 0:
            src = sum_out.at[s, share(c, peer), :]
            dst = sum_in.at[s, k - 1, slot(c), :]
        else:
            src = total.at[s, share(c, layer), :]
            dst = src
        return remote(
            src, dst, sum_sem.at[s, c, phase, 0, k - 1], sum_sem.at[s, c, phase, 1, k - 1],
            "layer", peer,
        )

    def sum_first(s, c):
        sum_out[s, span(c), :] = part[s, span(c), :].astype(BF16)
        for k in (2, 1, 3):
            sum_copy(s, c, 0, k).start()

    def sum_second(s, c):
        for k in range(1, peers):
            sum_copy(s, c, 0, k).wait_recv()
        mine = share(c, layer)
        value = part[s, mine, :]
        for k in range(1, peers):
            value = value + sum_in[s, k - 1, slot(c), :].astype(F32)
        total[s, mine, :] = value.astype(BF16)
        for k in (2, 1, 3):
            sum_copy(s, c, 1, k).start()

    def sum_third(s, c):
        for k in range(1, peers):
            sum_copy(s, c, 1, k).wait_recv()

    def sum_finish(s, c):
        for k in range(1, peers):
            sum_copy(s, c, 0, k).wait_send()
            sum_copy(s, c, 1, k).wait_send()

    def use_act(c, b):
        value = dot(full[b, span(c), :], enc_rows(b))
        part[0, span(c), :] = value if b is me else part[0, span(c), :] + value

    def use_err(c, b):
        value = dot(err[b, span(c), :], dec_columns(b), ((1,), (1,)))
        part[1, span(c), :] = value if b is me else part[1, span(c), :] + value

    def activate(c):
        sum_third(0, c)
        wide = 4.0 * (total[0, span(c), :].astype(F32) + benc_ref[...])
        soft = jnp.maximum(wide, 0.0) + jnp.log1p(jnp.exp(-jnp.abs(wide)))
        feat[span(c), :] = (soft * 0.25).astype(BF16)

    def open_gate(c):
        wide = 4.0 * (total[0, span(c), :].astype(F32) + benc_ref[...])
        gate[span(c), :] = scale * jax.nn.sigmoid(wide)

    def term(c, b):
        return dot(feat[span(c), :], dec_columns(b))

    def side_copy(c, at):
        return remote(
            side_out.at[at, span(c), :], side_in.at[at, span(c), :],
            side_sem.at[0, c, at], side_sem.at[1, c, at], "latent", partner,
        )

    def land(at, up):
        return at + 1 if up else at

    def line_copy(c, at, up):
        sems = up_sem if up else down_sem
        return remote(
            line_out.at[at, span(c), :], line_in.at[land(at, up), span(c), :], sems.at[0, c, at], sems.at[1, c, at],
            "latent", me + INNER if up else me - INNER,
        )

    def cross_copy(c, up):
        out, land, sems = (xup_out, xup_in, xup_sem) if up else (xdown_out, xdown_in, xdown_sem)
        return remote(
            out.at[span(c), :], land.at[span(c), :], sems.at[0, c], sems.at[1, c],
            "latent", me + INNER if up else me - INNER,
        )

    def at_distance(d, up, use):
        at = z + d if up else z - d
        pl.when(at < depth if up else at >= 0)(lambda: use(at))

    def scatter_other(c, d, up):
        def go(at):
            value = term(c, at * INNER + 1 - y).astype(BF16)
            if direct(c) and d == 1:
                out = xup_out if up else xdown_out
                out[span(c), :] = value
                cross_copy(c, up).start()
            else:
                side_out[at, span(c), :] = value
                side_copy(c, at).start()

        at_distance(d, up, go)

    def scatter_other_near(c):
        value = term(c, z * INNER + 1 - y)
        if not direct(c):
            side_out[z, span(c), :] = value.astype(BF16)
            side_copy(c, z).start()
            return
        own[z, span(c), :] = value
        for up, valid in ((True, not_bottom), (False, not_top)):

            @pl.when(valid)
            def _():
                cross_copy(c, up).wait_recv()
                own[z, span(c), :] = own[z, span(c), :] + (xup_in if up else xdown_in)[span(c), :].astype(F32)

        side_out[z, span(c), :] = own[z, span(c), :].astype(BF16)
        side_copy(c, z).start()

    def scatter_own(c, d, up):
        def go(at):
            own[at, span(c), :] = term(c, at * INNER + y)

        at_distance(d, up, go)

    def scatter_line(c, d, up):
        inner = not_bottom if up else not_top

        def go(at):
            value = own[at, span(c), :]
            if not (direct(c) and d == 1):
                side_copy(c, at).wait_recv()
                value = value + side_in[at, span(c), :].astype(F32)

            @pl.when(inner)
            def _():
                line_copy(c, at, up).wait_recv()
                line_out[at, span(c), :] = (
                    value + line_in[land(at, up), span(c), :].astype(F32)
                ).astype(BF16)

            @pl.when(jnp.logical_not(inner))
            def _():
                line_out[at, span(c), :] = value.astype(BF16)

            line_copy(c, at, up).start()

        at_distance(d, up, go)

    def scatter_last(c):
        side_copy(c, z).wait_recv()
        value = own[z, span(c), :] + side_in[z, span(c), :].astype(F32)
        own[z, span(c), :] = value + bdec_ref[...].astype(F32) - full[me, span(c), :].astype(F32)
        for up, valid in ((True, not_bottom), (False, not_top)):

            @pl.when(valid)
            def _():
                line_copy(c, z, up).wait_recv()
                own[z, span(c), :] = own[z, span(c), :] + line_in[land(z, up), span(c), :].astype(F32)

        value = own[z, span(c), :].astype(BF16)
        err[me, span(c), :] = value
        gbdec[...] = gbdec[...] + scale * jnp.sum(value.astype(F32), axis=0, keepdims=True)

    def scatter_finish(c):
        for d in range(depth - 1, 0, -1):
            for up in (True, False):
                if direct(c) and d == 1:
                    at_distance(d, up, lambda at: cross_copy(c, up).wait_send())
                else:
                    at_distance(d, up, lambda at: side_copy(c, at).wait_send())
                at_distance(d, up, lambda at: line_copy(c, at, up).wait_send())
        side_copy(c, z).wait_send()

    def close(c):
        sum_third(1, c)
        value = total[1, span(c), :].astype(F32) * gate[span(c), :]
        gbenc[...] = gbenc[...] + jnp.sum(value, axis=0, keepdims=True)
        gpre[span(c), :] = value.astype(BF16)

    def own_near(c):
        own[z, span(c), :] = term(c, z * INNER + y)

    def turn(b):
        turned[pl.ds(b * width, width), :] = full[b].T

    def turn_feat():
        feat_turned[...] = feat[...].T

    def finish_dec(b):
        columns = pl.ds(b * width, width)
        gdec[:, columns] = (scale * dot(feat_turned[...], err[b])).astype(BF16)

    def finish_enc(b):
        lines = pl.ds(b * width, width)
        genc[lines, :] = dot(turned[lines, :], gpre[...]).astype(BF16)

    source = lambda c: acts_hbm.at[span(c), :]
    event(0.05, loads[0].wait)
    event(0.06, loads[3].wait)
    event(2.0, loads[1].wait)
    event(2.0, loads[2].wait)
    event(2.0, loads[4].wait)
    last = closing = 0.0
    gap = plan["gap"]
    for c in range(chunks):
        ready = gather_events(
            full, ag_send, ag_recv, c, source(c), plan["act"][c], plan["act_hop"], use_act
        )
        last = max(last, ready)
        event(ready, sum_first, 0, c)
        event(ready + gap[0], sum_second, 0, c)
        event(ready + gap[0] + gap[1], activate, c)
        begin = max(ready + gap[0] + gap[1] + 0.05, plan["out"][c])
        hop = plan["out_hop"]
        for d in range(depth - 1, 0, -1):
            for up in (True, False):
                event(begin, scatter_other, c, d, up)
        for d in range(depth - 1, 0, -1):
            for up in (True, False):
                event(begin + 0.2, scatter_own, c, d, up)
                event(begin + 0.5 + (depth - d) * hop, scatter_line, c, d, up)
        event(begin + (plan["near"] if direct(c) else 0.3), scatter_other_near, c)
        own_time = max(begin + hop, begin + plan["near"]) + 0.1
        event(own_time, own_near, c)
        event(own_time + 0.1, open_gate, c)
        done = max(begin + 0.6 + depth * hop, own_time + 0.2)
        event(done, scatter_last, c)
        begin = max(done + 0.05, plan["err"][c])
        ready = gather_events(
            err, eg_send, eg_recv, c, None, begin, plan["err_hop"], use_err
        )
        event(ready, sum_first, 1, c)
        event(ready + gap[0], sum_second, 1, c)
        event(ready + gap[0] + gap[1], close, c)
        closing = max(closing, ready)
    if flat:
        for b in range(n):
            event(last + 2.0 + b, turn, b)
            event(closing + (0.01 if b < n // 2 else gap[0] + 0.01), finish_dec, b)
            event(closing + gap[0] + gap[1] + 1.0, finish_enc, b)
        event(closing - 1.0, turn_feat)
    for _, _, function in sorted(events, key=lambda e: e[:2]):
        function()
    for c in range(chunks):
        gather_finish(full, ag_send, ag_recv, c, source(c))
        gather_finish(err, eg_send, eg_recv, c, None)
        scatter_finish(c)
        for s in range(2):
            sum_finish(s, c)


def body(n, acts, w_enc, b_enc, w_dec, b_dec):
    local, enc, dec = acts[0], w_enc[0], w_dec[0]
    tokens, width = local.shape
    latents = enc.shape[1]
    depth = n // INNER
    flat = width % 128 == 0 and latents % 128 == 0
    unit = tokens // sum(SHARES)
    if flat and tokens % sum(SHARES) == 0 and unit % 64 == 0:
        sizes, plan = [unit * s for s in SHARES], PLAN
    else:
        sizes, plan = [tokens], SINGLE
    chunks = len(sizes)
    scale = tokens ** (-0.5)
    if not flat:
        dec = dec.reshape(latents, n, width).transpose(1, 0, 2)
    vmem = pl.BlockSpec(memory_space=pltpu.VMEM)
    hbm = pl.BlockSpec(memory_space=pl.ANY)
    dma = pltpu.SemaphoreType.DMA
    blocks = (n, tokens, width)
    hidden = (tokens, latents)
    side = pltpu.VMEM((depth, tokens, width), BF16)
    line = pltpu.VMEM((depth + 1, tokens, width), BF16)
    cross = pltpu.VMEM((tokens, width), BF16)
    small = (jax.ShapeDtypeStruct((1, latents), F32), jax.ShapeDtypeStruct((1, width), F32))
    inner = (blocks, blocks, hidden, hidden)
    if flat:
        outs = (pltpu.VMEM((n * width, latents), BF16), pltpu.VMEM((latents, n * width), BF16))
        extra = [pltpu.VMEM(shape, BF16) for shape in inner]
        extra += [pltpu.VMEM((n * width, tokens), BF16), pltpu.VMEM((latents, tokens), BF16)]
    else:
        outs = tuple(jax.ShapeDtypeStruct(shape, BF16) for shape in inner)
        extra = []
    results = pl.pallas_call(
        functools.partial(step_kernel, n, sizes, plan, flat, scale),
        out_shape=outs + small,
        in_specs=[hbm] * 5,
        out_specs=(vmem,) * (len(outs) + 2),
        scratch_shapes=extra + [
            pltpu.VMEM(enc.shape, BF16),
            pltpu.VMEM(dec.shape, BF16),
            pltpu.VMEM((1, latents), F32),
            pltpu.VMEM((1, width), BF16),
            pltpu.VMEM((2,) + hidden, F32),
            pltpu.VMEM((depth, tokens, width), F32),
            side, side, line, line,
            cross, cross, cross, cross,
            pltpu.VMEM((2,) + hidden, BF16),
            pltpu.VMEM((2, 3, tokens // 4, latents), BF16),
            pltpu.VMEM((2,) + hidden, BF16),
            pltpu.VMEM(hidden, F32),
            dma((5,)),
            dma((chunks, n, 3)),
            dma((chunks, n)),
            dma((chunks, n, 3)),
            dma((chunks, n)),
            dma((2, chunks, depth)),
            dma((2, chunks, depth)),
            dma((2, chunks, depth)),
            dma((2, chunks)),
            dma((2, chunks)),
            dma((2, chunks, 2, 2, 3)),
        ],
        compiler_params=pltpu.CompilerParams(
            collective_id=0, has_side_effects=True,
            vmem_limit_bytes=VMEM_LIMIT - (4 * n * width * latents if flat else 0),
        ),
        name="step",
    )(local, enc, dec, b_enc[None, :], b_dec)
    gbenc, gbdec = results[-2:]
    if flat:
        genc, gdec = results[:2]
    else:
        full, err, feat, gpre = results[:4]
        genc = jnp.einsum("btw,tl->bwl", full, gpre, preferred_element_type=F32)
        genc = genc.astype(BF16).reshape(n * width, latents)
        gdec = jnp.einsum("tl,btw->lbw", feat, err, preferred_element_type=F32)
        gdec = (scale * gdec).astype(BF16).reshape(latents, n * width)
    return genc[None], gdec[None], gbenc[0], gbdec


def solution(mesh):
    return jax.shard_map(
        functools.partial(body, mesh.shape["latent"]),
        mesh=mesh,
        in_specs=(
            P("layer", None, "latent"),
            P("layer", None, "latent"),
            P("latent"),
            P("layer", "latent", None),
            P("layer", "latent"),
        ),
        out_specs=(
            P("layer", None, "latent"),
            P("layer", "latent", None),
            P("latent"),
            P("layer", "latent"),
        ),
        check_vma=False,
    )
```

time: 164 us -> 103 us (0.63)
  Pallas kernels: 132 us -> 98.6 us
  matrix products: 17.5 us -> 0 us
  other arithmetic: 7.63 us -> 0 us
    pallas_call x5 -> x1, Pallas kernels: 132 us -> 98.6 us  [body(): pl.pallas_call(functools.partial(step_kernel, n, sizes, plan, flat, scale...]
    dot_general x5 -> x0, matrix products: 17.5 us -> none  [the longest x1 4.34 us: body(): lax.dot_general(feat, err, (((0,), (0,)), ((), ())), preferred_element_ty...]
    convert_element_type x3 -> x0, other arithmetic: 4.45 us -> none  [the longest x2 2.75 us: body(): feat = (jax.nn.softplus(4.0 * pre) / 4.0).astype(BF16)]
    reduce_sum x2 -> x0, other arithmetic: 2.54 us -> none  [the longest x1 2.16 us: body(): grad_benc = jnp.sum(grad_pre, axis=0)]
    unnamed x13 -> x8, local copies, waits for them, and re-layouts: 3.95 us -> 3.79 us
where the time goes in v1:
time: 103 us
  Pallas kernels  98.6 us (96%)
  local copies, waits for them, and re-layouts  3.79 us (4%)
    pallas_call x1, Pallas kernels, body(): pl.pallas_call(functools.partial(step_kernel, n, sizes, plan, flat, scale...  98.6 us
    unnamed x8, local copies, waits for them, and re-layouts  3.79 us

profile of v1, /device:TPU:0, one launch (start us, length us, event | category | flops | bytes accessed | tf_op | source)
XLA Modules:
  0.0 103.1 jit_solution(6981930601566852189)
XLA Ops:
  0.6 98.6 %step.1 = (bf16[2048,512]{1,0:T(8,128)(2,1)S(1)}, bf16[512,2048]{1,0:T(8,128)(2,1)S(1)}, f32[1,512]{1,0:T(1,128)}, f32[1,256]{1,0:T(1,128)}) custom-call(bf16[512,256]{1,0:T(8,128)(2,1)} %bitcast.11, bf16[2048,512]{1,0:T(8,128)(2,1)} %bitcast.9, bf16[512,2048]{1,0:T(8,128)(2,1)} %bitcast.10, f32[1,512]{1,0:T(1,128)} %bitcast.12, bf16[1,256]{1,0:T(2,128)(2,1)} %bdec_hbm.1), custom_call_target="tpu_custom_call" | custom-call | tf_op jit(solution)/shard_map/step/pallas_call | solution.py:483
  99.3 1.3 %copy.13 = bf16[1,2048,512]{2,1,0:T(8,128)(2,1)} copy(bf16[1,2048,512]{2,1,0:T(8,128)(2,1)S(1)} %bitcast.8) | data formatting | bytes 4194304
  100.6 0.0 copy-start
  100.6 0.0 copy-start.1
  100.6 1.3 %copy.14 = bf16[1,512,2048]{2,1,0:T(8,128)(2,1)} copy(bf16[1,512,2048]{2,1,0:T(8,128)(2,1)S(1)} %bitcast.7) | data formatting | bytes 4194304
  101.9 0.0 copy-done
  101.9 0.6 copy.15
  102.5 0.0 copy-done.1
  102.5 0.6 copy.16
Async XLA Ops:
  100.6 1.3 %copy-start = (f32[1,512]{1,0:T(1,128)S(1)}, f32[1,512]{1,0:T(1,128)}, u32[]{:S(2)}) copy-start(f32[1,512]{1,0:T(1,128)} %get-tuple-element.10) | copy-start | bytes 6148
  100.6 1.9 %copy-start.1 = (f32[1,256]{1,0:T(1,128)S(1)}, f32[1,256]{1,0:T(1,128)}, u32[]{:S(2)}) copy-start(f32[1,256]{1,0:T(1,128)} %get-tuple-element.23) | copy-start | bytes 3076

commit v2 on v1

--- a/solution.py
+++ b/solution.py
@@ -12,15 +12,68 @@
 BF16 = jnp.bfloat16
 INNER = 2
 VMEM_LIMIT = 60 * 1024 * 1024
-SHARES = (2, 2, 2, 1, 1)
-PLAN = dict(
-    direct=(0, 3), act=(0.0, 4.0, 9.0, 13.0, 16.0), act_hop=3.0, use=0.3, gap=(3.0, 3.0),
-    out=(16.0, 21.0, 27.0, 33.0, 36.0), out_hop=3.0, near=3.0, err=(0.0,) * 5, err_hop=3.0,
-)
-SINGLE = dict(
-    direct=(), act=(0.0,), act_hop=3.0, use=0.3, gap=(3.0, 3.0),
-    out=(0.0,), out_hop=3.0, near=3.0, err=(0.0,), err_hop=3.0,
-)
+SHARES = (1, 1, 1, 1)
+PLAN = {'use': 1.03,
+ 'chunks': [{'act': (0, [0.0, 1.0, 1.8], [5.9, 3.3, 6.0, 4.8]),
+             'sums': (9.4, 10.3),
+             'out': 6.9,
+             'line': [3.4, 36.6, 40.6],
+             'near': 30.8,
+             'own': 53.6,
+             'done': 4.0,
+             'err': (26.9, [60.7, 68.1, 79.3], [90.0, 87.1, 110.9, 102.0]),
+             'last_sums': (16.7, 28.3),
+             'cross': (False, True, False),
+             'chain': (3, 1, 3)},
+            {'act': (0, [0.9, 1.4, 2.6], [0.0, 7.4, 9.9, 8.6]),
+             'sums': (8.8, 10.0),
+             'out': 42.5,
+             'line': [58.3, 47.9, 34.1],
+             'near': 13.2,
+             'own': 8.6,
+             'done': 66.5,
+             'err': (10.6, [83.9, 98.4, 82.9], [96.5, 126.6, 125.6, 107.4]),
+             'last_sums': (23.3, 87.6),
+             'cross': (False, False, False),
+             'chain': (3, 1, 2)},
+            {'act': (0.1, [1.7, 10.1, 12.4], [21.6, 29.3, 26.5, 25.6]),
+             'sums': (15.1, 14.9),
+             'out': 50.9,
+             'line': [0.5, 2.6, 27.9],
+             'near': 41.5,
+             'own': 73.2,
+             'done': 39.1,
+             'err': (12.0, [112.8, 131.1, 102.9], [135.0, 132.8, 188.2, 128.9]),
+             'last_sums': (38.2, 7.0),
+             'cross': (True, False, False),
+             'chain': (3, 1, 2)},
+            {'act': (2.7, [11.1, 25.0, 18.6], [18.6, 42.2, 49.5, 36.5]),
+             'sums': (10.2, 7.1),
+             'out': 65.6,
+             'line': [87.7, 10.4, 68.0],
+             'near': 24.8,
+             'own': 87.4,
+             'done': 115.6,
+             'err': (101.3, [159.3, 148.8, 140.7], [145.7, 194.6, 202.3, 191.1]),
+             'last_sums': (25.1, 64.5),
+             'cross': (True, False, True),
+             'chain': (2, 2, 1)}]}
+
+
+def default_plan(depth, chunks):
+    plan = []
+    for c in range(chunks):
+        begin, hop = 4.0 * c, 3.0
+        act = begin, [begin + d * hop for d in range(1, depth)], [begin + (d + 1) * hop for d in range(depth)]
+        out = begin + (depth + 3) * hop
+        done = out + (depth + 1) * hop
+        err = done, [done + d * hop for d in range(1, depth)], [done + (d + 1) * hop for d in range(depth)]
+        plan.append(dict(
+            act=act, sums=(hop, hop), out=out, line=[out + (depth - d) * hop for d in range(1, depth)],
+            near=out + 0.3, own=out + hop, done=done, err=err, last_sums=(hop, hop),
+            cross=(False, False, False), chain=(depth - 1,) * 3,
+        ))
+    return dict(use=0.3, chunks=plan)
 
 
 def remote(src, dst, send, recv, axis, index):
@@ -40,16 +93,15 @@
 
 def step_kernel(n, sizes, plan, flat, scale, acts_hbm, enc_hbm, dec_hbm, benc_hbm, bdec_hbm, *refs):
     if flat:
-        (genc, gdec, gbenc, gbdec), refs = refs[:4], refs[4:]
-        (full, err, feat, gpre, turned, feat_turned), refs = refs[:6], refs[6:]
+        (turned, gpre, gdec, gbenc, gbdec), refs = refs[:5], refs[5:]
+        (full, err, feat, feat_turned), refs = refs[:4], refs[4:]
     else:
         (full, err, feat, gpre, gbenc, gbdec), refs = refs[:6], refs[6:]
     (
         enc, dec, benc_ref, bdec_ref, part, own,
         side_out, side_in, line_out, line_in,
         xup_out, xup_in, xdown_out, xdown_in, sum_out, sum_in, total, gate,
-        load_sem, ag_send, ag_recv, eg_send, eg_recv,
-        side_sem, up_sem, down_sem, xup_sem, xdown_sem, sum_sem,
+        far_in, load_sem, block_send, block_recv, side_sem, line_send, line_recv, cross_sem, far_recv, sum_sem,
     ) = refs
     depth = n // INNER
     tokens, width = acts_hbm.shape
@@ -92,8 +144,7 @@
     def span(c):
         return pl.ds(starts[c], sizes[c])
 
-    def direct(c):
-        return c in plan["direct"]
+    steps = plan["chunks"]
 
     def share(c, peer):
         quarter = sizes[c] // peers
@@ -112,52 +163,86 @@
 
     targets = (partner, me + INNER, me - INNER)
 
-    def gather_copy(buf, send, recv, c, b, way, source=None):
+    def at_distance(d, up, use):
+        at = z + d if up else z - d
+        pl.when(at < depth if up else at >= 0)(lambda: use(at))
+
+    def gather_copy(buf, c, b, way, source=None):
         spot = buf.at[b, span(c), :]
         return remote(
             spot if source is None else source, spot,
-            send.at[c, b, way], recv.at[c, b], "latent", targets[way],
-        )
-
-    def gather_own(buf, send, recv, c, source, act):
-        def go(way):
-            act(gather_copy(buf, send, recv, c, me, way, source))
-
-        pl.when(not_top)(lambda: go(1))
-        pl.when(not_bottom)(lambda: go(2))
-        go(0)
-
-    def gather_line(buf, send, recv, c, d, below, act, wait):
-        at = z - d if below else z + d
-
-        @pl.when(at >= 0 if below else at < depth)
-        def _():
+            block_send.at[c, b], block_recv.at[c, b], "latent", targets[way],
+        )
+
+    def gather_far(buf, c, at, source):
+        spot = buf.at[me, span(c), :]
+        return remote(
+            spot if source is None else source, spot,
+            block_send.at[c, me], block_recv.at[c, me], "latent", at * INNER + y,
+        )
+
+    def drain(buf, c, b, count, most):
+        for k in range(1, most + 1):
+
+            @pl.when(count == k)
+            def _():
+                spot = buf.at[pl.ds(0, k), span(c), :]
+                remote(
+                    spot, spot, block_send.at[c, b], block_recv.at[c, b], "latent", partner
+                ).wait_send()
+
+    def gather_own(buf, c, chain, source):
+        for d in range(depth - 1, chain, -1):
+            for up in (True, False):
+                at_distance(d, up, lambda at: gather_far(buf, c, at, source).start())
+        pl.when(not_top)(lambda: gather_copy(buf, c, me, 1, source).start())
+        pl.when(not_bottom)(lambda: gather_copy(buf, c, me, 2, source).start())
+        gather_copy(buf, c, me, 0, source).start()
+
+    def gather_line(buf, c, cross, chain, d, below):
+        def go(at):
             b = at * INNER + y
-            if wait:
-                gather_copy(buf, send, recv, c, b, 0).wait_recv()
-            way = 1 if below else 2
-
-            @pl.when(not_top if below else not_bottom)
-            def _():
-                act(gather_copy(buf, send, recv, c, b, way))
-
-            if not (direct(c) and d == 1):
-                act(gather_copy(buf, send, recv, c, b, 0))
-
-    def gather_side(buf, send, recv, c, d, below, act, wait):
-        at = z - d if below else z + d
-
-        @pl.when(at >= 0 if below else at < depth)
-        def _():
+            gather_copy(buf, c, b, 0).wait_recv()
+            if d < chain:
+                way = 1 if below else 2
+                pl.when(not_top if below else not_bottom)(lambda: gather_copy(buf, c, b, way).start())
+            if not (cross and d == 1):
+                gather_copy(buf, c, b, 0).start()
+
+        at_distance(d, not below, go)
+
+    def gather_side(buf, c, cross, d, below):
+        def go(at):
             b = at * INNER + 1 - y
-            if wait:
-                gather_copy(buf, send, recv, c, b, 0).wait_recv()
-            if direct(c) and d == 0:
-                for way, valid in ((1, not_top), (2, not_bottom)):
-
-                    @pl.when(valid)
-                    def _():
-                        act(gather_copy(buf, send, recv, c, b, way))
+            gather_copy(buf, c, b, 0).wait_recv()
+            if cross and d == 0:
+                pl.when(not_top)(lambda: gather_copy(buf, c, b, 1).start())
+                pl.when(not_bottom)(lambda: gather_copy(buf, c, b, 2).start())
+
+        at_distance(d, not below, go)
+
+    def one(condition):
+        return jnp.where(condition, 1, 0)
+
+    def gather_drain(buf, c, cross, chain):
+        ends = one(not_top) + one(not_bottom)
+        count = 1 + ends
+        for d in range(chain + 1, depth):
+            count = count + one(z + d < depth) + one(z >= d)
+        drain(buf, c, me, count, depth + 1)
+        for d in range(1, depth):
+            for below in (True, False):
+
+                def go(at):
+                    count = 0 if cross and d == 1 else 1
+                    if d < chain:
+                        count = count + one(not_top if below else not_bottom)
+                    drain(buf, c, at * INNER + y, count, 2)
+
+                if d < chain or not (cross and d == 1):
+                    at_distance(d, not below, go)
+        if cross:
+            drain(buf, c, partner, ends, 2)
 
     def on_block(d, below, side, use):
         at = z - d if below else z + d
@@ -166,38 +251,30 @@
         def _():
             use(at * INNER + (1 - y if side else y))
 
-    def start(copy):
-        copy.start()
-
-    def finish(copy):
-        copy.wait_send()
-
     events = []
 
     def event(time, function, *args):
         events.append((time, len(events), functools.partial(function, *args)))
 
-    def gather_events(buf, send, recv, c, source, time, hop, use):
-        event(time, gather_own, buf, send, recv, c, source, start)
-        event(time + 0.1, use, c, me)
+    def gather_events(buf, c, cross, chain, source, times, use):
+        begin, along, aside = times
+        late = plan["use"]
+        event(begin, gather_own, buf, c, chain, source)
+        event(begin + 0.1, use, c, me)
+        last = begin + 0.1
         for d in range(1, depth):
+            at = max(along[d - 1], begin + 0.2)
+            last = max(last, at + late)
             for below in (True, False):
-                at = time + d * hop
-                event(at, gather_line, buf, send, recv, c, d, below, start, True)
-                event(at + plan["use"], on_block, d, below, False, functools.partial(use, c))
+                event(at, gather_line, buf, c, cross, chain, d, below)
+                event(at + late, on_block, d, below, False, functools.partial(use, c))
         for d in range(depth):
+            at = max(aside[d], begin + 0.2)
+            last = max(last, at + late)
             for below in (True, False) if d else (True,):
-                at = time + (d + 1) * hop + 0.2
-                event(at, gather_side, buf, send, recv, c, d, below, start, True)
-                event(at + 0.3, on_block, d, below, True, functools.partial(use, c))
-        return time + depth * hop + 0.6
-
-    def gather_finish(buf, send, recv, c, source):
-        gather_own(buf, send, recv, c, source, finish)
-        for d in range(1, depth):
-            for below in (True, False):
-                gather_line(buf, send, recv, c, d, below, finish, False)
-        gather_side(buf, send, recv, c, 0, True, finish, False)
+                event(at, gather_side, buf, c, cross, d, below)
+                event(at + late, on_block, d, below, True, functools.partial(use, c))
+        return last + 0.05
 
     def sum_copy(s, c, phase, k):
         peer = lax.rem(layer + k, peers)
@@ -208,8 +285,14 @@
             src = total.at[s, share(c, layer), :]
             dst = src
         return remote(
-            src, dst, sum_sem.at[s, c, phase, 0, k - 1], sum_sem.at[s, c, phase, 1, k - 1],
-            "layer", peer,
+            src, dst, sum_sem.at[0, c, phase], sum_sem.at[1, c, phase], "layer", peer,
+        )
+
+    def sum_all(s, c, phase):
+        spot = sum_in.at[s, :, slot(c), :]
+        return remote(
+            spot, spot, sum_sem.at[0, c, phase], sum_sem.at[1, c, phase], "layer",
+            lax.rem(layer + 1, peers),
         )
 
     def sum_first(s, c):
@@ -218,8 +301,7 @@
             sum_copy(s, c, 0, k).start()
 
     def sum_second(s, c):
-        for k in range(1, peers):
-            sum_copy(s, c, 0, k).wait_recv()
+        sum_all(s, c, 0).wait_recv()
         mine = share(c, layer)
         value = part[s, mine, :]
         for k in range(1, peers):
@@ -229,13 +311,11 @@
             sum_copy(s, c, 1, k).start()
 
     def sum_third(s, c):
-        for k in range(1, peers):
-            sum_copy(s, c, 1, k).wait_recv()
+        sum_all(s, c, 1).wait_recv()
 
     def sum_finish(s, c):
-        for k in range(1, peers):
-            sum_copy(s, c, 0, k).wait_send()
-            sum_copy(s, c, 1, k).wait_send()
+        sum_all(s, c, 0).wait_send()
+        sum_all(s, c, 1).wait_send()
 
     def use_act(c, b):
         value = dot(full[b, span(c), :], enc_rows(b))
@@ -268,27 +348,30 @@
         return at + 1 if up else at
 
     def line_copy(c, at, up):
-        sems = up_sem if up else down_sem
-        return remote(
-            line_out.at[at, span(c), :], line_in.at[land(at, up), span(c), :], sems.at[0, c, at], sems.at[1, c, at],
+        return remote(
+            line_out.at[at, span(c), :], line_in.at[land(at, up), span(c), :],
+            line_send.at[c, at], line_recv.at[c, land(at, up)],
             "latent", me + INNER if up else me - INNER,
         )
 
+    def far_copy(c, at, source):
+        return remote(
+            line_out.at[at, span(c), :], far_in.at[source, span(c), :],
+            line_send.at[c, at], far_recv.at[c, source], "latent", at * INNER + y,
+        )
+
     def cross_copy(c, up):
-        out, land, sems = (xup_out, xup_in, xup_sem) if up else (xdown_out, xdown_in, xdown_sem)
-        return remote(
-            out.at[span(c), :], land.at[span(c), :], sems.at[0, c], sems.at[1, c],
+        out, spot = (xup_out, xup_in) if up else (xdown_out, xdown_in)
+        k = 0 if up else 1
+        return remote(
+            out.at[span(c), :], spot.at[span(c), :], cross_sem.at[0, c, k], cross_sem.at[1, c, k],
             "latent", me + INNER if up else me - INNER,
         )
-
-    def at_distance(d, up, use):
-        at = z + d if up else z - d
-        pl.when(at < depth if up else at >= 0)(lambda: use(at))
 
     def scatter_other(c, d, up):
         def go(at):
             value = term(c, at * INNER + 1 - y).astype(BF16)
-            if direct(c) and d == 1:
+            if steps[c]["cross"][1] and d == 1:
                 out = xup_out if up else xdown_out
                 out[span(c), :] = value
                 cross_copy(c, up).start()
@@ -300,7 +383,7 @@
 
     def scatter_other_near(c):
         value = term(c, z * INNER + 1 - y)
-        if not direct(c):
+        if not steps[c]["cross"][1]:
             side_out[z, span(c), :] = value.astype(BF16)
             side_copy(c, z).start()
             return
@@ -326,9 +409,15 @@
 
         def go(at):
             value = own[at, span(c), :]
-            if not (direct(c) and d == 1):
+            if not (steps[c]["cross"][1] and d == 1):
                 side_copy(c, at).wait_recv()
                 value = value + side_in[at, span(c), :].astype(F32)
+
+            chain = steps[c]["chain"][1]
+            if d >= chain:
+                line_out[at, span(c), :] = value.astype(BF16)
+                (line_copy(c, at, up) if d == chain else far_copy(c, at, z)).start()
+                return
 
             @pl.when(inner)
             def _():
@@ -356,6 +445,14 @@
                 line_copy(c, z, up).wait_recv()
                 own[z, span(c), :] = own[z, span(c), :] + line_in[land(z, up), span(c), :].astype(F32)
 
+        for d in range(steps[c]["chain"][1] + 1, depth):
+            for up in (True, False):
+
+                def add(at):
+                    far_copy(c, z, at).wait_recv()
+                    own[z, span(c), :] = own[z, span(c), :] + far_in[at, span(c), :].astype(F32)
+
+                at_distance(d, up, add)
         value = own[z, span(c), :].astype(BF16)
         err[me, span(c), :] = value
         gbdec[...] = gbdec[...] + scale * jnp.sum(value.astype(F32), axis=0, keepdims=True)
@@ -363,11 +460,14 @@
     def scatter_finish(c):
         for d in range(depth - 1, 0, -1):
             for up in (True, False):
-                if direct(c) and d == 1:
+                if steps[c]["cross"][1] and d == 1:
                     at_distance(d, up, lambda at: cross_copy(c, up).wait_send())
                 else:
                     at_distance(d, up, lambda at: side_copy(c, at).wait_send())
-                at_distance(d, up, lambda at: line_copy(c, at, up).wait_send())
+                if d > steps[c]["chain"][1]:
+                    at_distance(d, up, lambda at: far_copy(c, at, z).wait_send())
+                else:
+                    at_distance(d, up, lambda at: line_copy(c, at, up).wait_send())
         side_copy(c, z).wait_send()
 
     def close(c):
@@ -388,10 +488,6 @@
     def finish_dec(b):
         columns = pl.ds(b * width, width)
         gdec[:, columns] = (scale * dot(feat_turned[...], err[b])).astype(BF16)
-
-    def finish_enc(b):
-        lines = pl.ds(b * width, width)
-        genc[lines, :] = dot(turned[lines, :], gpre[...]).astype(BF16)
 
     source = lambda c: acts_hbm.at[span(c), :]
     event(0.05, loads[0].wait)
@@ -400,52 +496,73 @@
     event(2.0, loads[2].wait)
     event(2.0, loads[4].wait)
     last = closing = 0.0
-    gap = plan["gap"]
     for c in range(chunks):
+        step = steps[c]
         ready = gather_events(
-            full, ag_send, ag_recv, c, source(c), plan["act"][c], plan["act_hop"], use_act
+            full, c, step["cross"][0], step["chain"][0], source(c), step["act"], use_act
+
         )
         last = max(last, ready)
+        first, second = step["sums"]
         event(ready, sum_first, 0, c)
-        event(ready + gap[0], sum_second, 0, c)
-        event(ready + gap[0] + gap[1], activate, c)
-        begin = max(ready + gap[0] + gap[1] + 0.05, plan["out"][c])
-        hop = plan["out_hop"]
+        event(ready + first, sum_second, 0, c)
+        event(ready + first + second, activate, c)
+        begin = max(ready + first + second + 0.05, step["out"])
         for d in range(depth - 1, 0, -1):
             for up in (True, False):
                 event(begin, scatter_other, c, d, up)
         for d in range(depth - 1, 0, -1):
             for up in (True, False):
                 event(begin + 0.2, scatter_own, c, d, up)
-                event(begin + 0.5 + (depth - d) * hop, scatter_line, c, d, up)
-        event(begin + (plan["near"] if direct(c) else 0.3), scatter_other_near, c)
-        own_time = max(begin + hop, begin + plan["near"]) + 0.1
-        event(own_time, own_near, c)
-        event(own_time + 0.1, open_gate, c)
-        done = max(begin + 0.6 + depth * hop, own_time + 0.2)
+                event(max(step["line"][d - 1], begin + 0.3), scatter_line, c, d, up)
+        near = max(step["near"], begin + 0.1)
+        event(near, scatter_other_near, c)
+        mine = max(step["own"], near + 0.01)
+        event(mine, own_near, c)
+        event(mine, open_gate, c)
+        done = max(step["done"], mine + 0.01)
+        event(done - 0.005, gather_drain, full, c, step["cross"][0], step["chain"][0])
         event(done, scatter_last, c)
-        begin = max(done + 0.05, plan["err"][c])
+        event(done + 0.005, sum_finish, 0, c)
+        times = step["err"]
         ready = gather_events(
-            err, eg_send, eg_recv, c, None, begin, plan["err_hop"], use_err
-        )
+            err, c, step["cross"][2], step["chain"][2], None,
+            (max(times[0], done + 0.01),) + tuple(times[1:]), use_err
+        )
+        first, second = step["last_sums"]
         event(ready, sum_first, 1, c)
-        event(ready + gap[0], sum_second, 1, c)
-        event(ready + gap[0] + gap[1], close, c)
+        event(ready + first, sum_second, 1, c)
+        event(ready + first + second, close, c)
         closing = max(closing, ready)
     if flat:
         for b in range(n):
             event(last + 2.0 + b, turn, b)
-            event(closing + (0.01 if b < n // 2 else gap[0] + 0.01), finish_dec, b)
-            event(closing + gap[0] + gap[1] + 1.0, finish_enc, b)
+            event(closing + (0.01 if b < n // 2 else first + 0.01), finish_dec, b)
         event(closing - 1.0, turn_feat)
     for _, _, function in sorted(events, key=lambda e: e[:2]):
         function()
     for c in range(chunks):
-        gather_finish(full, ag_send, ag_recv, c, source(c))
-        gather_finish(err, eg_send, eg_recv, c, None)
+        gather_drain(err, c, steps[c]["cross"][2], steps[c]["chain"][2])
         scatter_finish(c)
-        for s in range(2):
-            sum_finish(s, c)
+        sum_finish(1, c)
+
+
+def write_kernel(n, width, turned, gpre, gdec, gbenc, gbdec, genc_out, gdec_out, gbenc_out, gbdec_out, genc, sem):
+    copies = [
+        pltpu.make_async_copy(src, dst, sem.at[n + i])
+        for i, (src, dst) in enumerate(
+            ((gdec, gdec_out), (gbenc, gbenc_out), (gbdec, gbdec_out))
+        )
+    ]
+    for copy in copies:
+        copy.start()
+    for b in range(n):
+        lines = pl.ds(b * width, width)
+        genc[lines, :] = dot(turned[lines, :], gpre[...]).astype(BF16)
+        copies.append(pltpu.make_async_copy(genc.at[lines, :], genc_out.at[lines, :], sem.at[b]))
+        copies[-1].start()
+    for copy in copies:
+        copy.wait()
 
 
 def body(n, acts, w_enc, b_enc, w_dec, b_dec):
@@ -456,10 +573,14 @@
     flat = width % 128 == 0 and latents % 128 == 0
     unit = tokens // sum(SHARES)
     if flat and tokens % sum(SHARES) == 0 and unit % 64 == 0:
-        sizes, plan = [unit * s for s in SHARES], PLAN
+        sizes = [unit * s for s in SHARES]
     else:
-        sizes, plan = [tokens], SINGLE
+        sizes = [tokens]
     chunks = len(sizes)
+    plan = default_plan(depth, chunks)
+    if PLAN is not None and chunks == len(SHARES) and depth == len(PLAN["chunks"][0]["line"]) + 1:
+        plan = PLAN
+    far = any(step["chain"][1] < depth - 1 for step in plan["chunks"])
     scale = tokens ** (-0.5)
     if not flat:
         dec = dec.reshape(latents, n, width).transpose(1, 0, 2)
@@ -471,12 +592,16 @@
     side = pltpu.VMEM((depth, tokens, width), BF16)
     line = pltpu.VMEM((depth + 1, tokens, width), BF16)
     cross = pltpu.VMEM((tokens, width), BF16)
-    small = (jax.ShapeDtypeStruct((1, latents), F32), jax.ShapeDtypeStruct((1, width), F32))
+    kind = pltpu.VMEM if flat else jax.ShapeDtypeStruct
+    small = (kind((1, latents), F32), kind((1, width), F32))
     inner = (blocks, blocks, hidden, hidden)
     if flat:
-        outs = (pltpu.VMEM((n * width, latents), BF16), pltpu.VMEM((latents, n * width), BF16))
-        extra = [pltpu.VMEM(shape, BF16) for shape in inner]
-        extra += [pltpu.VMEM((n * width, tokens), BF16), pltpu.VMEM((latents, tokens), BF16)]
+        outs = (
+            pltpu.VMEM((n * width, tokens), BF16),
+            pltpu.VMEM(hidden, BF16),
+            pltpu.VMEM((latents, n * width), BF16),
+        )
+        extra = [pltpu.VMEM(shape, BF16) for shape in (blocks, blocks, hidden, (latents, tokens))]
     else:
         outs = tuple(jax.ShapeDtypeStruct(shape, BF16) for shape in inner)
         extra = []
@@ -498,17 +623,16 @@
             pltpu.VMEM((2, 3, tokens // 4, latents), BF16),
             pltpu.VMEM((2,) + hidden, BF16),
             pltpu.VMEM(hidden, F32),
+            side if far else pltpu.VMEM((1, 16, width), BF16),
             dma((5,)),
-            dma((chunks, n, 3)),
             dma((chunks, n)),
-            dma((chunks, n, 3)),
             dma((chunks, n)),
             dma((2, chunks, depth)),
-            dma((2, chunks, depth)),
-            dma((2, chunks, depth)),
-            dma((2, chunks)),
-            dma((2, chunks)),
-            dma((2, chunks, 2, 2, 3)),
+            dma((chunks, depth)),
+            dma((chunks, depth + 1)),
+            dma((2, chunks, 2)),
+            dma((chunks, depth)),
+            dma((2, chunks, 2)),
         ],
         compiler_params=pltpu.CompilerParams(
             collective_id=0, has_side_effects=True,
@@ -518,7 +642,19 @@
     )(local, enc, dec, b_enc[None, :], b_dec)
     gbenc, gbdec = results[-2:]
     if flat:
-        genc, gdec = results[:2]
+        held = [pltpu.with_memory_space_constraint(r, pltpu.VMEM) for r in results]
+        genc, gdec, gbenc, gbdec = pl.pallas_call(
+            functools.partial(write_kernel, n, width),
+            out_shape=(
+                jax.ShapeDtypeStruct((n * width, latents), BF16),
+                jax.ShapeDtypeStruct((latents, n * width), BF16),
+            ) + tuple(jax.ShapeDtypeStruct(r.shape, F32) for r in results[-2:]),
+            in_specs=[vmem] * 5,
+            out_specs=(hbm,) * 4,
+            scratch_shapes=[pltpu.VMEM((n * width, latents), BF16), dma((n + 3,))],
+            compiler_params=pltpu.CompilerParams(vmem_limit_bytes=8 * n * width * latents),
+            name="write",
+        )(*held)
     else:
         full, err, feat, gpre = results[:4]
         genc = jnp.einsum("btw,tl->bwl", full, gpre, preferred_element_type=F32)

time: 103 us -> 88.7 us (0.86)
  Pallas kernels: 98.6 us -> 87.7 us
  local copies, waits for them, and re-layouts: 3.79 us -> 0 us
    pallas_call x1, Pallas kernels: 98.6 us -> 85.6 us  [body(): pl.pallas_call(functools.partial(step_kernel, n, sizes, plan, flat, scale...]
    unnamed x8 -> x0, local copies, waits for them, and re-layouts: 3.79 us -> none
    pallas_call x0 -> x1, Pallas kernels: none -> 2.12 us  [body(): pl.pallas_call(functools.partial(write_kernel, n, width), out_shape=(jax....]
where the time goes in v2:
time: 88.7 us; the launch traced here: 88.5 us
  Pallas kernels  87.7 us (99%)
    pallas_call x1, Pallas kernels, body(): pl.pallas_call(functools.partial(step_kernel, n, sizes, plan, flat, scale...  85.6 us
    pallas_call x1, Pallas kernels, body(): pl.pallas_call(functools.partial(write_kernel, n, width), out_shape=(jax....  2.12 us

profile of v2, /device:TPU:0, one launch (start us, length us, event | category | flops | bytes accessed | tf_op | source)
XLA Modules:
  0.0 88.5 jit_solution(6600523332194189050)
XLA Ops:
  0.6 85.6 %step.1 = (bf16[2048,512]{1,0:T(8,128)(2,1)S(1)}, bf16[512,512]{1,0:T(8,128)(2,1)S(1)}, bf16[512,2048]{1,0:T(8,128)(2,1)S(1)}, f32[1,512]{1,0:T(1,128)S(1)}, f32[1,256]{1,0:T(1,128)S(1)}) custom-call(bf16[512,256]{1,0:T(8,128)(2,1)} %bitcast.9, bf16[2048,512]{1,0:T(8,128)(2,1)} %bitcast.7, bf16[512,2048]{1,0:T(8,128)(2,1)} %bitcast.8, f32[1,512]{1,0:T(1,128)} %bitcast.10, ...), custom_call_target="tpu_custom_call" | custom-call | tf_op jit(solution)/shard_map/step/pallas_call | solution.py:608
  86.3 2.1 %write.1 = (bf16[2048,512]{1,0:T(8,128)(2,1)}, bf16[512,2048]{1,0:T(8,128)(2,1)}, f32[1,512]{1,0:T(1,128)}, f32[1,256]{1,0:T(1,128)}) custom-call(bf16[2048,512]{1,0:T(8,128)(2,1)S(1)} %get-tuple-element.13.turned, bf16[512,512]{1,0:T(8,128)(2,1)S(1)} %get-tuple-element.14.gpre, bf16[512,2048]{1,0:T(8,128)(2,1)S(1)} %get-tuple-element.15.gdec, ...), custom_call_target="tpu_custom_call" | custom-call | tf_op jit(solution)/shard_map/write/pallas_call | solution.py:646

commit v3 on v2

--- a/solution.py
+++ b/solution.py
@@ -13,51 +13,51 @@
 INNER = 2
 VMEM_LIMIT = 60 * 1024 * 1024
 SHARES = (1, 1, 1, 1)
-PLAN = {'use': 1.03,
- 'chunks': [{'act': (0, [0.0, 1.0, 1.8], [5.9, 3.3, 6.0, 4.8]),
-             'sums': (9.4, 10.3),
-             'out': 6.9,
-             'line': [3.4, 36.6, 40.6],
-             'near': 30.8,
-             'own': 53.6,
-             'done': 4.0,
-             'err': (26.9, [60.7, 68.1, 79.3], [90.0, 87.1, 110.9, 102.0]),
-             'last_sums': (16.7, 28.3),
+PLAN = {'use': 0.01,
+ 'chunks': [{'act': (0, [0.0, 1.0, 6.5], [7.0, 6.0, 9.2, 14.2]),
+             'sums': (7.3, 10.1),
+             'out': 30.7,
+             'line': [8.1, 46.6, 34.7],
+             'near': 42.7,
+             'own': 52.3,
+             'done': 43.2,
+             'err': (54.3, [56.0, 68.8, 78.6], [75.2, 73.6, 79.9, 90.1]),
+             'last_sums': (18.2, 59.2),
              'cross': (False, True, False),
              'chain': (3, 1, 3)},
-            {'act': (0, [0.9, 1.4, 2.6], [0.0, 7.4, 9.9, 8.6]),
-             'sums': (8.8, 10.0),
-             'out': 42.5,
-             'line': [58.3, 47.9, 34.1],
-             'near': 13.2,
-             'own': 8.6,
-             'done': 66.5,
-             'err': (10.6, [83.9, 98.4, 82.9], [96.5, 126.6, 125.6, 107.4]),
-             'last_sums': (23.3, 87.6),
+            {'act': (0, [0.5, 3.8, 9.8], [5.2, 12.5, 15.8, 17.7]),
+             'sums': (8.4, 7.1),
+             'out': 25.8,
+             'line': [47.5, 44.5, 43.7],
+             'near': 43.3,
+             'own': 47.7,
+             'done': 54.2,
+             'err': (47.7, [55.4, 65.8, 79.9], [73.1, 82.6, 93.9, 91.0]),
+             'last_sums': (20.2, 70.1),
+             'cross': (True, False, True),
+             'chain': (3, 2, 3)},
+            {'act': (5.4, [15.6, 24.3, 28.6], [15.3, 25.9, 33.1, 32.6]),
+             'sums': (3.8, 9.8),
+             'out': 0,
+             'line': [66.7, 54.1, 48.6],
+             'near': 0.3,
+             'own': 70.6,
+             'done': 5.3,
+             'err': (63.8, [81.1, 90.8, 104.6], [88.3, 109.4, 119.7, 125.6]),
+             'last_sums': (25.4, 34.7),
              'cross': (False, False, False),
-             'chain': (3, 1, 2)},
-            {'act': (0.1, [1.7, 10.1, 12.4], [21.6, 29.3, 26.5, 25.6]),
-             'sums': (15.1, 14.9),
-             'out': 50.9,
-             'line': [0.5, 2.6, 27.9],
-             'near': 41.5,
-             'own': 73.2,
-             'done': 39.1,
-             'err': (12.0, [112.8, 131.1, 102.9], [135.0, 132.8, 188.2, 128.9]),
-             'last_sums': (38.2, 7.0),
-             'cross': (True, False, False),
-             'chain': (3, 1, 2)},
-            {'act': (2.7, [11.1, 25.0, 18.6], [18.6, 42.2, 49.5, 36.5]),
-             'sums': (10.2, 7.1),
-             'out': 65.6,
-             'line': [87.7, 10.4, 68.0],
-             'near': 24.8,
-             'own': 87.4,
-             'done': 115.6,
-             'err': (101.3, [159.3, 148.8, 140.7], [145.7, 194.6, 202.3, 191.1]),
-             'last_sums': (25.1, 64.5),
-             'cross': (True, False, True),
-             'chain': (2, 2, 1)}]}
+             'chain': (3, 2, 3)},
+            {'act': (0.7, [10.8, 17.7, 25.9], [41.8, 18.9, 26.5, 37.2]),
+             'sums': (5.1, 7.1),
+             'out': 7.2,
+             'line': [70.2, 58.1, 53.3],
+             'near': 28.8,
+             'own': 11.2,
+             'done': 78.9,
+             'err': (14.9, [89.5, 96.6, 111.9], [104.4, 137.9, 126.4, 146.6]),
+             'last_sums': (26.3, 18.6),
+             'cross': (False, False, True),
+             'chain': (3, 3, 3)}]}
 
 
 def default_plan(depth, chunks):
@@ -520,10 +520,10 @@
         mine = max(step["own"], near + 0.01)
         event(mine, own_near, c)
         event(mine, open_gate, c)
+        event(mine, gather_drain, full, c, step["cross"][0], step["chain"][0])
+        event(mine, sum_finish, 0, c)
         done = max(step["done"], mine + 0.01)
-        event(done - 0.005, gather_drain, full, c, step["cross"][0], step["chain"][0])
         event(done, scatter_last, c)
-        event(done + 0.005, sum_finish, 0, c)
         times = step["err"]
         ready = gather_events(
             err, c, step["cross"][2], step["chain"][2], None,
@@ -532,6 +532,8 @@
         first, second = step["last_sums"]
         event(ready, sum_first, 1, c)
         event(ready + first, sum_second, 1, c)
+        event(ready + first + 0.005, scatter_finish, c)
+        event(ready + first + 0.005, gather_drain, err, c, step["cross"][2], step["chain"][2])
         event(ready + first + second, close, c)
         closing = max(closing, ready)
     if flat:
@@ -542,8 +544,6 @@
     for _, _, function in sorted(events, key=lambda e: e[:2]):
         function()
     for c in range(chunks):
-        gather_drain(err, c, steps[c]["cross"][2], steps[c]["chain"][2])
-        scatter_finish(c)
         sum_finish(1, c)
 
 

time: 88.7 us -> 85.7 us (0.966)
  Pallas kernels: 87.7 us -> 84.7 us
    pallas_call x1, Pallas kernels: 85.6 us -> 82.6 us  [body(): pl.pallas_call(functools.partial(step_kernel, n, sizes, plan, flat, scale...]
where the time goes in v3:
time: 85.7 us; the launch traced here: 85.5 us
  Pallas kernels  84.7 us (99%)
    pallas_call x1, Pallas kernels, body(): pl.pallas_call(functools.partial(step_kernel, n, sizes, plan, flat, scale...  82.6 us
    pallas_call x1, Pallas kernels, body(): pl.pallas_call(functools.partial(write_kernel, n, width), out_shape=(jax....  2.12 us

profile of v3, /device:TPU:0, one launch (start us, length us, event | category | flops | bytes accessed | tf_op | source)
XLA Modules:
  0.0 85.5 jit_solution(17163429611918821204)
XLA Ops:
  0.6 82.6 %step.1 = (bf16[2048,512]{1,0:T(8,128)(2,1)S(1)}, bf16[512,512]{1,0:T(8,128)(2,1)S(1)}, bf16[512,2048]{1,0:T(8,128)(2,1)S(1)}, f32[1,512]{1,0:T(1,128)S(1)}, f32[1,256]{1,0:T(1,128)S(1)}) custom-call(bf16[512,256]{1,0:T(8,128)(2,1)} %bitcast.9, bf16[2048,512]{1,0:T(8,128)(2,1)} %bitcast.7, bf16[512,2048]{1,0:T(8,128)(2,1)} %bitcast.8, f32[1,512]{1,0:T(1,128)} %bitcast.10, ...), custom_call_target="tpu_custom_call" | custom-call | tf_op jit(solution)/shard_map/step/pallas_call | solution.py:608
  83.2 2.1 %write.1 = (bf16[2048,512]{1,0:T(8,128)(2,1)}, bf16[512,2048]{1,0:T(8,128)(2,1)}, f32[1,512]{1,0:T(1,128)}, f32[1,256]{1,0:T(1,128)}) custom-call(bf16[2048,512]{1,0:T(8,128)(2,1)S(1)} %get-tuple-element.13.turned, bf16[512,512]{1,0:T(8,128)(2,1)S(1)} %get-tuple-element.14.gpre, bf16[512,2048]{1,0:T(8,128)(2,1)S(1)} %get-tuple-element.15.gdec, ...), custom_call_target="tpu_custom_call" | custom-call | tf_op jit(solution)/shard_map/write/pallas_call | solution.py:646

commit v4 on v3

--- a/solution.py
+++ b/solution.py
@@ -14,50 +14,50 @@
 VMEM_LIMIT = 60 * 1024 * 1024
 SHARES = (1, 1, 1, 1)
 PLAN = {'use': 0.01,
- 'chunks': [{'act': (0, [0.0, 1.0, 6.5], [7.0, 6.0, 9.2, 14.2]),
-             'sums': (7.3, 10.1),
-             'out': 30.7,
-             'line': [8.1, 46.6, 34.7],
-             'near': 42.7,
-             'own': 52.3,
-             'done': 43.2,
-             'err': (54.3, [56.0, 68.8, 78.6], [75.2, 73.6, 79.9, 90.1]),
-             'last_sums': (18.2, 59.2),
-             'cross': (False, True, False),
+ 'chunks': [{'act': (3.4, [5.5, 18.8, 25.2], [21.1, 27.7, 28.9, 30.0]),
+             'sums': (0.2, 10.3, 4.1),
+             'out': 35.4,
+             'line': [9.2, 52.2, 56.5],
+             'near': 52.7,
+             'own': 60.0,
+             'done': 8.8,
+             'err': (14.6, [70.1, 77.1, 82.9], [91.1, 83.7, 97.0, 104.5]),
+             'last_sums': (6.2, 32.6, 42.9),
+             'cross': (True, True, False),
              'chain': (3, 1, 3)},
-            {'act': (0, [0.5, 3.8, 9.8], [5.2, 12.5, 15.8, 17.7]),
-             'sums': (8.4, 7.1),
-             'out': 25.8,
-             'line': [47.5, 44.5, 43.7],
-             'near': 43.3,
-             'own': 47.7,
-             'done': 54.2,
-             'err': (47.7, [55.4, 65.8, 79.9], [73.1, 82.6, 93.9, 91.0]),
-             'last_sums': (20.2, 70.1),
-             'cross': (True, False, True),
-             'chain': (3, 2, 3)},
-            {'act': (5.4, [15.6, 24.3, 28.6], [15.3, 25.9, 33.1, 32.6]),
-             'sums': (3.8, 9.8),
-             'out': 0,
-             'line': [66.7, 54.1, 48.6],
-             'near': 0.3,
-             'own': 70.6,
-             'done': 5.3,
-             'err': (63.8, [81.1, 90.8, 104.6], [88.3, 109.4, 119.7, 125.6]),
-             'last_sums': (25.4, 34.7),
+            {'act': (0, [4.5, 6.5, 12.2], [5.8, 8.4, 21.9, 23.5]),
+             'sums': (2.5, 4.1, 2.2),
+             'out': 21.8,
+             'line': [46.2, 44.5, 39.3],
+             'near': 23.3,
+             'own': 5.3,
+             'done': 55.5,
+             'err': (19.4, [57.4, 64.6, 81.1], [73.2, 80.4, 98.7, 97.8]),
+             'last_sums': (9.4, 32.9, 68.9),
              'cross': (False, False, False),
              'chain': (3, 2, 3)},
-            {'act': (0.7, [10.8, 17.7, 25.9], [41.8, 18.9, 26.5, 37.2]),
-             'sums': (5.1, 7.1),
-             'out': 7.2,
-             'line': [70.2, 58.1, 53.3],
-             'near': 28.8,
-             'own': 11.2,
-             'done': 78.9,
-             'err': (14.9, [89.5, 96.6, 111.9], [104.4, 137.9, 126.4, 146.6]),
-             'last_sums': (26.3, 18.6),
+            {'act': (0, [5.0, 9.5, 23.5], [21.5, 10.5, 27.9, 27.6]),
+             'sums': (6.4, 10.5, 3.2),
+             'out': 22.8,
+             'line': [71.2, 62.3, 57.2],
+             'near': 61.2,
+             'own': 78.8,
+             'done': 71.9,
+             'err': (3.3, [101.4, 110.7, 103.7], [102.7, 119.1, 134.1, 126.1]),
+             'last_sums': (37.7, 36.6, 34.2),
+             'cross': (False, True, False),
+             'chain': (3, 3, 2)},
+            {'act': (9.2, [25.7, 30.1, 31.9], [24.3, 44.0, 36.1, 43.7]),
+             'sums': (1.6, 5.6, 5.9),
+             'out': 37.2,
+             'line': [73.3, 68.1, 56.0],
+             'near': 41.6,
+             'own': 13.9,
+             'done': 82.0,
+             'err': (59.8, [107.1, 117.8, 119.3], [116.1, 173.1, 162.1, 179.1]),
+             'last_sums': (29.2, 9.7, 52.4),
              'cross': (False, False, True),
-             'chain': (3, 3, 3)}]}
+             'chain': (3, 3, 2)}]}
 
 
 def default_plan(depth, chunks):
@@ -69,8 +69,8 @@
         done = out + (depth + 1) * hop
         err = done, [done + d * hop for d in range(1, depth)], [done + (d + 1) * hop for d in range(depth)]
         plan.append(dict(
-            act=act, sums=(hop, hop), out=out, line=[out + (depth - d) * hop for d in range(1, depth)],
-            near=out + 0.3, own=out + hop, done=done, err=err, last_sums=(hop, hop),
+            act=act, sums=(hop / 2, hop, hop / 2), out=out, line=[out + (depth - d) * hop for d in range(1, depth)],
+            near=out + 0.3, own=out + hop, done=done, err=err, last_sums=(hop / 2, hop, hop / 2),
             cross=(False, False, False), chain=(depth - 1,) * 3,
         ))
     return dict(use=0.3, chunks=plan)
@@ -110,7 +110,8 @@
     z, y = me // INNER, lax.rem(me, INNER)
     partner = z * INNER + 1 - y
     layer = lax.axis_index("layer")
-    peers = 4
+    core = lax.rem(layer, 2)
+    twin, opposite = layer + 1 - 2 * core, lax.rem(layer + 2, 4)
     not_top, not_bottom = z < depth - 1, z > 0
 
     barrier = pltpu.get_barrier_semaphore()
@@ -121,8 +122,8 @@
     greet("latent", partner)
     pl.when(not_top)(lambda: greet("latent", me + INNER))
     pl.when(not_bottom)(lambda: greet("latent", me - INNER))
-    for k in range(1, peers):
-        greet("layer", lax.rem(layer + k, peers))
+    greet("layer", twin)
+    greet("layer", opposite)
     loads = [
         pltpu.make_async_copy(acts_hbm, full.at[me], load_sem.at[0]),
         pltpu.make_async_copy(benc_hbm, benc_ref, load_sem.at[1]),
@@ -133,7 +134,7 @@
     for load in loads:
         load.start()
     pl.semaphore_wait(
-        barrier, peers + jnp.where(not_top, 1, 0) + jnp.where(not_bottom, 1, 0)
+        barrier, 3 + jnp.where(not_top, 1, 0) + jnp.where(not_bottom, 1, 0)
     )
 
     gbdec[...] = jnp.zeros_like(gbdec)
@@ -146,12 +147,12 @@
 
     steps = plan["chunks"]
 
-    def share(c, peer):
-        quarter = sizes[c] // peers
-        return pl.ds(pl.multiple_of(starts[c] + peer * quarter, quarter), quarter)
+    def half(c, k):
+        size = sizes[c] // 2
+        return pl.ds(pl.multiple_of(starts[c] + k * size, size), size)
 
     def slot(c):
-        return pl.ds(starts[c] // peers, sizes[c] // peers)
+        return pl.ds(starts[c] // 2, sizes[c] // 2)
 
     def enc_rows(b):
         return enc[pl.ds(pl.multiple_of(b * width, width), width), :]
@@ -276,46 +277,41 @@
                 event(at + late, on_block, d, below, True, functools.partial(use, c))
         return last + 0.05
 
-    def sum_copy(s, c, phase, k):
-        peer = lax.rem(layer + k, peers)
+    def sum_copy(s, c, phase):
         if phase == 0:
-            src = sum_out.at[s, share(c, peer), :]
-            dst = sum_in.at[s, k - 1, slot(c), :]
+            src, dst = sum_out.at[s, half(c, 1 - core), :], sum_in.at[s, 0, slot(c), :]
+        elif phase == 1:
+            src, dst = sum_out.at[s, half(c, core), :], sum_in.at[s, 1, slot(c), :]
         else:
-            src = total.at[s, share(c, layer), :]
-            dst = src
+            src = dst = total.at[s, half(c, core), :]
+        mark = 3 if phase == 1 and s else phase
         return remote(
-            src, dst, sum_sem.at[0, c, phase], sum_sem.at[1, c, phase], "layer", peer,
-        )
-
-    def sum_all(s, c, phase):
-        spot = sum_in.at[s, :, slot(c), :]
-        return remote(
-            spot, spot, sum_sem.at[0, c, phase], sum_sem.at[1, c, phase], "layer",
-            lax.rem(layer + 1, peers),
+            src, dst, sum_sem.at[0, c, mark], sum_sem.at[1, c, mark],
+            "layer", opposite if phase == 1 else twin,
         )
 
     def sum_first(s, c):
-        sum_out[s, span(c), :] = part[s, span(c), :].astype(BF16)
-        for k in (2, 1, 3):
-            sum_copy(s, c, 0, k).start()
+        sum_out[s, half(c, 1 - core), :] = part[s, half(c, 1 - core), :].astype(BF16)
+        sum_copy(s, c, 0).start()
 
     def sum_second(s, c):
-        sum_all(s, c, 0).wait_recv()
-        mine = share(c, layer)
-        value = part[s, mine, :]
-        for k in range(1, peers):
-            value = value + sum_in[s, k - 1, slot(c), :].astype(F32)
-        total[s, mine, :] = value.astype(BF16)
-        for k in (2, 1, 3):
-            sum_copy(s, c, 1, k).start()
+        sum_copy(s, c, 0).wait_recv()
+        value = part[s, half(c, core), :] + sum_in[s, 0, slot(c), :].astype(F32)
+        sum_out[s, half(c, core), :] = value.astype(BF16)
+        sum_copy(s, c, 1).start()
 
     def sum_third(s, c):
-        sum_all(s, c, 1).wait_recv()
+        sum_copy(s, c, 1).wait_recv()
+        value = sum_out[s, half(c, core), :].astype(F32) + sum_in[s, 1, slot(c), :].astype(F32)
+        total[s, half(c, core), :] = value.astype(BF16)
+        sum_copy(s, c, 2).start()
+
+    def sum_fourth(s, c):
+        sum_copy(s, c, 2).wait_recv()
 
     def sum_finish(s, c):
-        sum_all(s, c, 0).wait_send()
-        sum_all(s, c, 1).wait_send()
+        for phase in range(3):
+            sum_copy(s, c, phase).wait_send()
 
     def use_act(c, b):
         value = dot(full[b, span(c), :], enc_rows(b))
@@ -326,7 +322,7 @@
         part[1, span(c), :] = value if b is me else part[1, span(c), :] + value
 
     def activate(c):
-        sum_third(0, c)
+        sum_fourth(0, c)
         wide = 4.0 * (total[0, span(c), :].astype(F32) + benc_ref[...])
         soft = jnp.maximum(wide, 0.0) + jnp.log1p(jnp.exp(-jnp.abs(wide)))
         feat[span(c), :] = (soft * 0.25).astype(BF16)
@@ -471,7 +467,7 @@
         side_copy(c, z).wait_send()
 
     def close(c):
-        sum_third(1, c)
+        sum_fourth(1, c)
         value = total[1, span(c), :].astype(F32) * gate[span(c), :]
         gbenc[...] = gbenc[...] + jnp.sum(value, axis=0, keepdims=True)
         gpre[span(c), :] = value.astype(BF16)
@@ -503,11 +499,13 @@
 
         )
         last = max(last, ready)
-        first, second = step["sums"]
+        first, second, third = step["sums"]
         event(ready, sum_first, 0, c)
         event(ready + first, sum_second, 0, c)
-        event(ready + first + second, activate, c)
-        begin = max(ready + first + second + 0.05, step["out"])
+        event(ready + first + second, sum_third, 0, c)
+        ready = ready + first + second + third
+        event(ready, activate, c)
+        begin = max(ready + 0.05, step["out"])
         for d in range(depth - 1, 0, -1):
             for up in (True, False):
                 event(begin, scatter_other, c, d, up)
@@ -529,17 +527,18 @@
             err, c, step["cross"][2], step["chain"][2], None,
             (max(times[0], done + 0.01),) + tuple(times[1:]), use_err
         )
-        first, second = step["last_sums"]
+        first, second, third = step["last_sums"]
         event(ready, sum_first, 1, c)
         event(ready + first, sum_second, 1, c)
         event(ready + first + 0.005, scatter_finish, c)
         event(ready + first + 0.005, gather_drain, err, c, step["cross"][2], step["chain"][2])
-        event(ready + first + second, close, c)
+        event(ready + first + second, sum_third, 1, c)
+        event(ready + first + second + third, close, c)
         closing = max(closing, ready)
     if flat:
         for b in range(n):
             event(last + 2.0 + b, turn, b)
-            event(closing + (0.01 if b < n // 2 else first + 0.01), finish_dec, b)
+            event(closing + 0.01 + (0.0 if b < n // 4 else first if b < 3 * n // 4 else first + second), finish_dec, b)
         event(closing - 1.0, turn_feat)
     for _, _, function in sorted(events, key=lambda e: e[:2]):
         function()
@@ -572,7 +571,7 @@
     depth = n // INNER
     flat = width % 128 == 0 and latents % 128 == 0
     unit = tokens // sum(SHARES)
-    if flat and tokens % sum(SHARES) == 0 and unit % 64 == 0:
+    if flat and tokens % sum(SHARES) == 0 and unit % 32 == 0:
         sizes = [unit * s for s in SHARES]
     else:
         sizes = [tokens]
@@ -620,7 +619,7 @@
             side, side, line, line,
             cross, cross, cross, cross,
             pltpu.VMEM((2,) + hidden, BF16),
-            pltpu.VMEM((2, 3, tokens // 4, latents), BF16),
+            pltpu.VMEM((2, 2, tokens // 2, latents), BF16),
             pltpu.VMEM((2,) + hidden, BF16),
             pltpu.VMEM(hidden, F32),
             side if far else pltpu.VMEM((1, 16, width), BF16),
@@ -632,7 +631,7 @@
             dma((chunks, depth + 1)),
             dma((2, chunks, 2)),
             dma((chunks, depth)),
-            dma((2, chunks, 2)),
+            dma((2, chunks, 4)),
         ],
         compiler_params=pltpu.CompilerParams(
             collective_id=0, has_side_effects=True,

time: 85.7 us -> 83.8 us (0.978)
  Pallas kernels: 84.7 us -> 82.9 us
    pallas_call x1, Pallas kernels: 82.6 us -> 80.7 us  [body(): pl.pallas_call(functools.partial(step_kernel, n, sizes, plan, flat, scale...]
where the time goes in v4:
time: 83.8 us; the launch traced here: 83.7 us
  Pallas kernels  82.9 us (99%)
    pallas_call x1, Pallas kernels, body(): pl.pallas_call(functools.partial(step_kernel, n, sizes, plan, flat, scale...  80.7 us
    pallas_call x1, Pallas kernels, body(): pl.pallas_call(functools.partial(write_kernel, n, width), out_shape=(jax....  2.12 us

profile of v4, /device:TPU:0, one launch (start us, length us, event | category | flops | bytes accessed | tf_op | source)
XLA Modules:
  0.0 83.7 jit_solution(6878224504680657045)
XLA Ops:
  0.6 80.7 %step.1 = (bf16[2048,512]{1,0:T(8,128)(2,1)S(1)}, bf16[512,512]{1,0:T(8,128)(2,1)S(1)}, bf16[512,2048]{1,0:T(8,128)(2,1)S(1)}, f32[1,512]{1,0:T(1,128)S(1)}, f32[1,256]{1,0:T(1,128)S(1)}) custom-call(bf16[512,256]{1,0:T(8,128)(2,1)} %bitcast.9, bf16[2048,512]{1,0:T(8,128)(2,1)} %bitcast.7, bf16[512,2048]{1,0:T(8,128)(2,1)} %bitcast.8, f32[1,512]{1,0:T(1,128)} %bitcast.10, ...), custom_call_target="tpu_custom_call" | custom-call | tf_op jit(solution)/shard_map/step/pallas_call | solution.py:607
  81.4 2.1 %write.1 = (bf16[2048,512]{1,0:T(8,128)(2,1)}, bf16[512,2048]{1,0:T(8,128)(2,1)}, f32[1,512]{1,0:T(1,128)}, f32[1,256]{1,0:T(1,128)}) custom-call(bf16[2048,512]{1,0:T(8,128)(2,1)S(1)} %get-tuple-element.13.turned, bf16[512,512]{1,0:T(8,128)(2,1)S(1)} %get-tuple-element.14.gpre, bf16[512,2048]{1,0:T(8,128)(2,1)S(1)} %get-tuple-element.15.gdec, ...), custom_call_target="tpu_custom_call" | custom-call | tf_op jit(solution)/shard_map/write/pallas_call | solution.py:645

commit v5 on v4

--- a/solution.py
+++ b/solution.py
@@ -13,49 +13,49 @@
 INNER = 2
 VMEM_LIMIT = 60 * 1024 * 1024
 SHARES = (1, 1, 1, 1)
-PLAN = {'use': 0.01,
- 'chunks': [{'act': (3.4, [5.5, 18.8, 25.2], [21.1, 27.7, 28.9, 30.0]),
-             'sums': (0.2, 10.3, 4.1),
-             'out': 35.4,
-             'line': [9.2, 52.2, 56.5],
-             'near': 52.7,
-             'own': 60.0,
-             'done': 8.8,
-             'err': (14.6, [70.1, 77.1, 82.9], [91.1, 83.7, 97.0, 104.5]),
-             'last_sums': (6.2, 32.6, 42.9),
+PLAN = {'use': 0.088,
+ 'chunks': [{'act': (1.653, [5.379, 17.95, 26.421], [20.826, 28.034, 28.439, 29.995]),
+             'sums': (0.08, 10.405, 3.909),
+             'out': 16.53,
+             'line': [24.781, 53.549, 55.87],
+             'near': 53.611,
+             'own': 66.352,
+             'done': 49.587,
+             'err': (8.342, [73.948, 77.397, 89.794], [94.104, 89.88, 98.665, 109.267]),
+             'last_sums': (10.487, 27.255, 56.675),
              'cross': (True, True, False),
              'chain': (3, 1, 3)},
-            {'act': (0, [4.5, 6.5, 12.2], [5.8, 8.4, 21.9, 23.5]),
-             'sums': (2.5, 4.1, 2.2),
-             'out': 21.8,
-             'line': [46.2, 44.5, 39.3],
-             'near': 23.3,
-             'own': 5.3,
-             'done': 55.5,
-             'err': (19.4, [57.4, 64.6, 81.1], [73.2, 80.4, 98.7, 97.8]),
-             'last_sums': (9.4, 32.9, 68.9),
+            {'act': (0, [1.872, 6.068, 14.928], [13.569, 14.243, 18.59, 23.119]),
+             'sums': (3.581, 3.316, 2.845),
+             'out': 29.289,
+             'line': [52.625, 44.425, 34.078],
+             'near': 24.318,
+             'own': 16.406,
+             'done': 55.534,
+             'err': (24.524, [66.338, 71.499, 85.811], [72.325, 95.07, 98.666, 103.516]),
+             'last_sums': (6.426, 25.889, 71.057),
              'cross': (False, False, False),
              'chain': (3, 2, 3)},
-            {'act': (0, [5.0, 9.5, 23.5], [21.5, 10.5, 27.9, 27.6]),
-             'sums': (6.4, 10.5, 3.2),
-             'out': 22.8,
-             'line': [71.2, 62.3, 57.2],
-             'near': 61.2,
-             'own': 78.8,
-             'done': 71.9,
-             'err': (3.3, [101.4, 110.7, 103.7], [102.7, 119.1, 134.1, 126.1]),
-             'last_sums': (37.7, 36.6, 34.2),
+            {'act': (1.53, [2.47, 9.524, 21.086], [16.35, 14.535, 27.595, 27.956]),
+             'sums': (5.982, 10.669, 8.185),
+             'out': 33.606,
+             'line': [76.416, 67.271, 61.011],
+             'near': 68.254,
+             'own': 85.726,
+             'done': 84.6,
+             'err': (3.093, [100.283, 111.038, 98.974], [103.821, 124.235, 144.106, 127.222]),
+             'last_sums': (37.069, 36.778, 50.644),
              'cross': (False, True, False),
              'chain': (3, 3, 2)},
-            {'act': (9.2, [25.7, 30.1, 31.9], [24.3, 44.0, 36.1, 43.7]),
-             'sums': (1.6, 5.6, 5.9),
-             'out': 37.2,
-             'line': [73.3, 68.1, 56.0],
-             'near': 41.6,
-             'own': 13.9,
-             'done': 82.0,
-             'err': (59.8, [107.1, 117.8, 119.3], [116.1, 173.1, 162.1, 179.1]),
-             'last_sums': (29.2, 9.7, 52.4),
+            {'act': (8.103, [26.698, 30.062, 32.555], [25.325, 40.634, 37.702, 43.001]),
+             'sums': (2.95, 7.984, 10.445),
+             'out': 44.006,
+             'line': [76.422, 72.264, 55.17],
+             'near': 11.685,
+             'own': 21.728,
+             'done': 87.738,
+             'err': (73.523, [107.214, 119.94, 123.367], [114.268, 171.21, 175.814, 183.56]),
+             'last_sums': (28.002, 6.534, 64.422),
              'cross': (False, False, True),
              'chain': (3, 3, 2)}]}
 
@@ -485,8 +485,8 @@
         columns = pl.ds(b * width, width)
         gdec[:, columns] = (scale * dot(feat_turned[...], err[b])).astype(BF16)
 
-    source = lambda c: acts_hbm.at[span(c), :]
-    event(0.05, loads[0].wait)
+    source = lambda c: None
+    event(-1.0, loads[0].wait)
     event(0.06, loads[3].wait)
     event(2.0, loads[1].wait)
     event(2.0, loads[2].wait)

time: 83.8 us -> 83.3 us (level)
  no operation moved by 1% of the time
where the time goes in v5:
time: 83.3 us; the launch traced here: 83.1 us
  Pallas kernels  82.3 us (99%)
    pallas_call x1, Pallas kernels, body(): pl.pallas_call(functools.partial(step_kernel, n, sizes, plan, flat, scale...  80.2 us
    pallas_call x1, Pallas kernels, body(): pl.pallas_call(functools.partial(write_kernel, n, width), out_shape=(jax....  2.12 us

profile of v5, /device:TPU:0, one launch (start us, length us, event | category | flops | bytes accessed | tf_op | source)
XLA Modules:
  0.0 83.1 jit_solution(73463903917537338)
XLA Ops:
  0.6 80.2 %step.1 = (bf16[2048,512]{1,0:T(8,128)(2,1)S(1)}, bf16[512,512]{1,0:T(8,128)(2,1)S(1)}, bf16[512,2048]{1,0:T(8,128)(2,1)S(1)}, f32[1,512]{1,0:T(1,128)S(1)}, f32[1,256]{1,0:T(1,128)S(1)}) custom-call(bf16[512,256]{1,0:T(8,128)(2,1)} %bitcast.9, bf16[2048,512]{1,0:T(8,128)(2,1)} %bitcast.7, bf16[512,2048]{1,0:T(8,128)(2,1)} %bitcast.8, f32[1,512]{1,0:T(1,128)} %bitcast.10, ...), custom_call_target="tpu_custom_call" | custom-call | tf_op jit(solution)/shard_map/step/pallas_call | solution.py:607
  80.9 2.1 %write.1 = (bf16[2048,512]{1,0:T(8,128)(2,1)}, bf16[512,2048]{1,0:T(8,128)(2,1)}, f32[1,512]{1,0:T(1,128)}, f32[1,256]{1,0:T(1,128)}) custom-call(bf16[2048,512]{1,0:T(8,128)(2,1)S(1)} %get-tuple-element.13.turned, bf16[512,512]{1,0:T(8,128)(2,1)S(1)} %get-tuple-element.14.gpre, bf16[512,2048]{1,0:T(8,128)(2,1)S(1)} %get-tuple-element.15.gdec, ...), custom_call_target="tpu_custom_call" | custom-call | tf_op jit(solution)/shard_map/write/pallas_call | solution.py:645
